TPU v7x, 32 devices: a whole 2x2x4 slice. The times are simulated.
32 devices in a mesh: gx: 8 (over z, core), gy: 2 (over x), ga: 2 (over y).
Axes of the slice: x: 2, y: 2, z: 4, core: 2. Of those that a mesh axis runs over, the one named last changes fastest.
Arguments:
- samples: bfloat16 [16, 64, 32, 512], P('ga', 'gx', 'gy'), parts along dimension 0, may hold values from -6 to 6
- model_prev: bfloat16 [16, 64, 32, 512], P('ga', 'gx', 'gy'), parts along dimension 0, may hold values from -6 to 6
- threshold: float32 [64, 32], P('gx', 'gy'), may hold values from 0.1 to 1
- support: int32 [64, 32, 256], P('gx', 'gy'), may hold values from 0 to 511
- sample_basis: bfloat16 [512, 64], replicated, may hold values from -0.25 to 0.25
- eval_basis: bfloat16 [64, 512], replicated, may hold values from -0.25 to 0.25
- transfer_x: bfloat16 [8, 8, 64, 64], replicated, may hold values from -0.25 to 0.25
- transfer_y: bfloat16 [2, 2, 64, 64], replicated, may hold values from -0.5 to 0.5
Outputs:
- model_next: float32 [16, 64, 32, 512], P('ga', 'gx', 'gy'), parts along dimension 0
- residual: bfloat16 [16, 64, 32, 512], P('ga', 'gx', 'gy'), parts along dimension 0
There are 2 independent parts, one for each index of `ga`. A program takes and returns all parts, laid end to end along the dimension named above; an argument that names none is the same for every part. Nothing has to cross between parts.
All inputs are finite; a program needn't handle non-finite values.
Results may differ from a plain program's by a relative error of at most 0.015.
Values may be sent and summed in bfloat16 or wider, within the bound.
No kernel may reach another device: no remote copies, remote signals or barrier semaphores. Data moves between devices by JAX's collectives and lax.ppermute only.
A program may use at most 64 MiB of HBM per device.

v0:
```python
import functools

import jax
import jax.numpy as jnp
from jax import lax
from jax.experimental import pallas as pl
from jax.experimental.pallas import tpu as pltpu
from jax.sharding import PartitionSpec as P


CHUNKS = 2
PIECES = 2
F32 = jnp.float32
BF16 = jnp.bfloat16


def mm(a, b):
    return lax.dot_general(a, b, (((1,), (0,)), ((), ())), preferred_element_type=F32)


def mm_nt(a, b):
    return lax.dot_general(a, b, (((1,), (1,)), ((), ())), preferred_element_type=F32)


def swap(x, axes, mesh_shape, masks):
    sizes = [mesh_shape[axis] for axis in axes]
    total = 1
    for size in sizes:
        total *= size
    pairs = []
    for source in range(total):
        rest, coords = source, []
        for size in reversed(sizes):
            coords.append(rest % size)
            rest //= size
        coords.reverse()
        target = 0
        for coord, mask, size in zip(coords, masks, sizes):
            target = target * size + (coord ^ mask)
        pairs.append((source, target))
    return lax.ppermute(x, axes, pairs)


VMEM = pl.BlockSpec(memory_space=pltpu.VMEM)
ANY = pl.BlockSpec(memory_space=pl.ANY)
PARAMS = pltpu.CompilerParams(vmem_limit_bytes=8 << 20)


def coeff_kernel(*refs):
    model_hbm, samples_hbm, eval_hbm, basis_hbm = refs[:4]
    outs = refs[4:-4]
    model_ref, samples_ref, weight_ref, sems = refs[-4:]
    k = eval_hbm.shape[0]
    pieces, step = model_ref.shape[:2]
    copies = [
        pltpu.make_async_copy(eval_hbm, weight_ref.at[pl.ds(0, k)], sems.at[0]),
        pltpu.make_async_copy(basis_hbm, weight_ref.at[pl.ds(k, k)], sems.at[1]),
    ]
    for i in range(pieces):
        part = pl.ds(i * step, step)
        copies.append(pltpu.make_async_copy(model_hbm.at[part], model_ref.at[i], sems.at[2 + 2 * i]))
        copies.append(pltpu.make_async_copy(samples_hbm.at[part], samples_ref.at[i], sems.at[3 + 2 * i]))
    for copy in copies:
        copy.start()
    copies[0].wait()
    copies[1].wait()
    weights = weight_ref[...].T
    lane = lax.broadcasted_iota(jnp.int32, (step, 2 * k), 1)
    for i in range(pieces):
        copies[2 + 2 * i].wait()
        copies[3 + 2 * i].wait()
        top = mm(model_ref[i], weights)
        low = mm(samples_ref[i], weights)
        out_ref = outs[i * len(outs) // pieces]
        row = i * step % out_ref.shape[0]
        out_ref[row : row + step] = jnp.where(lane < k, top, low).astype(BF16)


def coefficients(model, samples, evals, basis_t, chunks):
    rows, width = model.shape
    k = evals.shape[0]
    pieces = chunks * PIECES if rows % (16 * chunks * PIECES) == 0 else chunks
    return pl.pallas_call(
        coeff_kernel,
        in_specs=[ANY] * 4,
        out_specs=[VMEM] * chunks,
        out_shape=[pltpu.VMEM((rows // chunks, 2 * k), BF16)] * chunks,
        scratch_shapes=[
            pltpu.VMEM((pieces, rows // pieces, width), BF16),
            pltpu.VMEM((pieces, rows // pieces, width), BF16),
            pltpu.VMEM((2 * k, width), BF16),
            pltpu.SemaphoreType.DMA((2 + 2 * pieces,)),
        ],
        cost_estimate=pl.CostEstimate(
            flops=8 * rows * width * k, bytes_accessed=4 * rows * (width + k), transcendentals=0
        ),
        name="coefficients",
    )(model, samples, evals, basis_t)


def table_kernel(n_gy, near, tx_ref, ty_ref, basis_ref, out_ref):
    k = basis_ref.shape[0]
    own_x, own_y = lax.axis_index("gx"), lax.axis_index("gy")
    targets = (own_x, own_x ^ near)
    flat = tx_ref.shape[1] * k

    def turned(s):
        return tx_ref[s].reshape(flat, k).T

    span = 4
    stacked = jnp.concatenate([basis_ref[...]] * span, axis=0)
    gram = mm_nt(stacked, stacked)
    row = lax.broadcasted_iota(jnp.int32, gram.shape, 0) // k
    col = lax.broadcasted_iota(jnp.int32, gram.shape, 1) // k
    gram = jnp.where(row == col, gram, 0.0).astype(BF16)
    turned_sources = [turned(own_x ^ m) for m in range(near)]
    to_targets = jnp.concatenate([turned_sources[0], turned(targets[1])], axis=0)
    y_turned = jnp.concatenate([ty_ref[s].reshape(n_gy * k, k).T for s in range(n_gy)], axis=0)
    step = span * k
    weighted = jnp.concatenate(
        [
            mm(to_targets[:, i : i + step], gram).astype(BF16)
            for i in range(0, to_targets.shape[1], step)
        ],
        axis=1,
    )
    sources = jnp.concatenate(turned_sources, axis=0)
    cross = mm_nt(sources, weighted).astype(BF16)
    zero = jnp.zeros((k, k), BF16)

    def pair(block):
        return jnp.concatenate(
            [jnp.concatenate([block, zero], axis=1), jnp.concatenate([zero, block], axis=1)], axis=0
        )

    inner = [mm(cross, pair(ty_ref[own_y, m])).astype(BF16) for m in range(n_gy)]
    lane = lax.broadcasted_iota(jnp.int32, (k, 2 * k), 1)
    for m in range(near):
        source = own_x ^ m
        stacked_inner = jnp.concatenate([part[m * k : (m + 1) * k] for part in inner], axis=0)
        normal = mm(y_turned, stacked_inner)
        to_rows = jnp.concatenate([tx_ref[source, t] for t in targets], axis=0)
        from_rows = jnp.concatenate([tx_ref[t, source] for t in targets], axis=0)
        for s in range(n_gy):
            forward = mm_nt(ty_ref[s, own_y].T, to_rows)
            back = mm(from_rows, jnp.concatenate([ty_ref[own_y, s]] * 2, axis=1))
            negated = normal[s * k : (s + 1) * k]
            slot = (s ^ own_y) * near + m
            first = jnp.where(lane < k, forward, -jnp.roll(negated, k, axis=1))
            second = jnp.where(lane < k, jnp.roll(forward, k, axis=1), -negated)
            out_ref[slot, :k, : 2 * k] = first.astype(BF16)
            out_ref[slot, :k, 2 * k :] = second.astype(BF16)
            for i in range(2):
                adjoint = jnp.where(lane < k, 0.0, back[i * k : (i + 1) * k])
                out_ref[slot, k:, 2 * k * i : 2 * k * (i + 1)] = adjoint.astype(BF16)


def make_tables(n_gy, near, transfer_x, transfer_y, basis_t):
    k = transfer_x.shape[3]
    return pl.pallas_call(
        functools.partial(table_kernel, n_gy, near),
        in_specs=[VMEM] * 3,
        out_specs=VMEM,
        out_shape=jax.ShapeDtypeStruct((n_gy * near, 2 * k, 4 * k), BF16),
        cost_estimate=pl.CostEstimate(
            flops=200000000, bytes_accessed=2000000, transcendentals=0
        ),
        compiler_params=PARAMS,
        name="tables",
    )(transfer_x, transfer_y, basis_t)


def mask_kernel(support_ref, threshold_ref, out_ref):
    count = out_ref.shape[1]
    picked = support_ref[...].T
    word, bit = picked >> 5, jnp.int32(1) << (picked & 31)
    words = count // 32
    index = lax.broadcasted_iota(jnp.int32, (words, picked.shape[1]), 0)
    bits = jnp.zeros(index.shape, jnp.int32)
    for j in range(picked.shape[0]):
        bits = bits | jnp.where(index == word[j : j + 1], bit[j : j + 1], 0)
    shift = lax.broadcasted_iota(jnp.int32, (32, picked.shape[1]), 0)
    flags = jnp.concatenate([(bits[w : w + 1] >> shift) & 1 for w in range(words)], axis=0)
    kept = flags.T != 0
    levels = threshold_ref[...].T
    ly = levels.shape[0]
    for i in range(levels.shape[1]):
        rows = slice(i * ly, (i + 1) * ly)
        out_ref[rows] = jnp.where(kept[rows], levels[:, i : i + 1], jnp.inf)


def threshold_map(support, threshold, width):
    boxes = support.shape[0]
    return pl.pallas_call(
        mask_kernel,
        in_specs=[VMEM] * 2,
        out_specs=VMEM,
        out_shape=jax.ShapeDtypeStruct((boxes, width), F32),
        cost_estimate=pl.CostEstimate(
            flops=boxes * width * 32, bytes_accessed=4 * boxes * width, transcendentals=0
        ),
        compiler_params=PARAMS,
        name="threshold_map",
    )(support, threshold)


def mix_kernel(count, *refs):
    tables_ref, far_ref, own_ref = refs[count:]
    k2 = refs[0].shape[1]
    tables = tables_ref[...].reshape(count * k2, 2 * k2)
    for i in range(0, refs[0].shape[0], 256):
        mixed = mm(jnp.concatenate([ref[i : i + 256] for ref in refs[:count]], axis=1), tables)
        own_ref[i : i + 256] = mixed[:, :k2]
        far_ref[i : i + 256] = mixed[:, k2:].astype(BF16)


def mix(parts, tables):
    rows, k2 = parts[0].shape
    count = len(parts)
    return pl.pallas_call(
        functools.partial(mix_kernel, count),
        in_specs=[VMEM] * (count + 1),
        out_specs=[VMEM, VMEM],
        out_shape=[
            jax.ShapeDtypeStruct((rows, k2), BF16),
            jax.ShapeDtypeStruct((rows, k2), F32),
        ],
        cost_estimate=pl.CostEstimate(
            flops=4 * rows * count * k2 * k2,
            bytes_accessed=2 * rows * k2 * count,
            transcendentals=0,
        ),
        compiler_params=PARAMS,
        name="mix",
    )(*parts, tables)


def finish_kernel(first, *refs):
    own_ref, far_ref, model_ref, samples_ref, limit_ref, eval_ref, basis_ref = refs[:7]
    next_ref, residual_ref = refs[-2:]
    zero = jnp.zeros(eval_ref.shape, BF16)
    to_data = jnp.concatenate([basis_ref[...], zero], axis=0)
    to_model = jnp.concatenate([zero, eval_ref[...]], axis=0)
    limit = limit_ref[...]
    boxes = limit.shape[0]
    start = pl.program_id(0) * next_ref.shape[0]
    for i in range(0, next_ref.shape[0], boxes):
        here = pl.multiple_of(start + i, boxes)
        rows, whole = pl.ds(here, boxes), pl.ds(first + here, boxes)
        both = (own_ref[rows] + far_ref[rows].astype(F32)).astype(BF16)
        predicted = mm(both, to_data)
        residual_ref[i : i + boxes] = (samples_ref[whole].astype(F32) - predicted).astype(BF16)
        stepped = model_ref[whole].astype(F32) + mm(both, to_model)
        next_ref[i : i + boxes] = stepped - jnp.minimum(jnp.maximum(stepped, -limit), limit)


def finish(own, far, model, samples, limit, evals, basis_t, first, earlier):
    total, width = model.shape
    rows, k2 = own.shape
    block = limit.shape[0]
    skip = first // block
    wide = pl.BlockSpec((block, width), lambda i: (i + skip, 0))
    return pl.pallas_call(
        functools.partial(finish_kernel, first),
        grid=(rows // block,),
        in_specs=[VMEM] * 7 + [ANY] * len(earlier),
        out_specs=[wide, wide],
        out_shape=[
            jax.ShapeDtypeStruct((total, width), F32),
            jax.ShapeDtypeStruct((total, width), BF16),
        ],
        input_output_aliases={7 + i: i for i in range(len(earlier))},
        cost_estimate=pl.CostEstimate(
            flops=4 * rows * width * k2, bytes_accessed=10 * rows * width, transcendentals=0
        ),
        compiler_params=PARAMS,
        name="finish",
    )(own, far, model, samples, limit, evals, basis_t, *earlier)


def on_device(mesh_shape, samples, model_prev, threshold, support, sample_basis, eval_basis, transfer_x, transfer_y):
    n_gx, n_gy = mesh_shape["gx"], mesh_shape["gy"]
    near = n_gx // 2
    gathers, lx, ly, width = model_prev.shape
    boxes = lx * ly
    rows = gathers * boxes
    basis_t = sample_basis.T
    model = model_prev.reshape(rows, width)
    data = samples.reshape(rows, width)
    chunks = CHUNKS if gathers % CHUNKS == 0 else 1
    size = rows // chunks
    axes = ("gx", "gy")

    near_parts = []
    all_coeffs = coefficients(model, data, eval_basis, basis_t, chunks)
    for coeffs in all_coeffs:
        parts = {}
        for my in reversed(range(n_gy)):
            for mx in reversed(range(0, near, 2)):
                parts[my, mx] = swap(coeffs, axes, mesh_shape, (mx, my)) if mx or my else coeffs
        near_parts.append(parts)
    tables = make_tables(n_gy, near, transfer_x, transfer_y, basis_t)
    limit = threshold_map(
        support.reshape(boxes, support.shape[2]), threshold, width
    )
    mixed = []
    for parts in near_parts:
        for my in range(n_gy):
            for mx in range(0, near, 2):
                parts[my, mx + 1] = swap(parts[my, mx], axes, mesh_shape, (1, 0))
        ordered = [parts[my, mx] for my in range(n_gy) for mx in range(near)]
        far, own = mix(ordered, tables)
        mixed.append((own, swap(far, axes, mesh_shape, (near, 0))))
    outs = ()
    for c, (own, far) in enumerate(mixed):
        outs = finish(own, far, model, data, limit, eval_basis, basis_t, c * size, outs)
    model_next, residual = outs
    return model_next.reshape(model_prev.shape), residual.reshape(samples.shape)


def step(mesh_shape, *args):
    return on_device(mesh_shape, *args)


def solution(mesh):
    return jax.shard_map(
        functools.partial(step, dict(mesh.shape)),
        mesh=mesh,
        in_specs=(
            P("ga", "gx", "gy", None),
            P("ga", "gx", "gy", None),
            P("gx", "gy"),
            P("gx", "gy", None),
            P(),
            P(),
            P(),
            P(),
        ),
        out_specs=(P("ga", "gx", "gy", None), P("ga", "gx", "gy", None)),
        check_vma=False,
    )
```

profile of v0, /device:TPU:0, one launch (start us, length us, event | category | flops | bytes accessed | tf_op | source)
XLA Modules:
  0.0 39.7 jit_solution(13245765450850230184)
XLA Ops:
  0.7 2.5 %coefficients.1 = (bf16[512,128]{1,0:T(8,128)(2,1)S(1)}, bf16[512,128]{1,0:T(8,128)(2,1)S(1)}) custom-call(bf16[1024,512]{1,0:T(8,128)(2,1)} %bitcast.6, bf16[1024,512]{1,0:T(8,128)(2,1)} %bitcast.9, bf16[64,512]{1,0:T(8,128)(2,1)} %refs_5_.3, bf16[64,512]{1,0:T(8,128)(2,1)} %bitcast.12), custom_call_target="tpu_custom_call" | custom-call | flops 268435456 | bytes 2359296 | tf_op jit(solution)/shard_map/coefficients/pallas_call | solution.py:83
  3.2 4.0 %collective-permute-start.5 = (bf16[512,128]{1,0:T(8,128)(2,1)S(1)}, bf16[512,128]{1,0:T(8,128)(2,1)S(1)}, u32[]{:S(2)}, u32[]{:S(2)}) collective-permute-start(bf16[512,128]{1,0:T(8,128)(2,1)S(1)} %get-tuple-element.12.refs_0_), channel_id=1, source_target_pairs={{0,10},{2,8},{4,14},{6,12},{8,2},{10,0},{12,6},{14,4},{16,26},{18,... | collective-permute-start | bytes 393224 | tf_op jit(solution)/shard_map/ppermute | solution.py:41
  7.2 0.6 %collective-permute-start.3 = (bf16[512,128]{1,0:T(8,128)(2,1)S(1)}, bf16[512,128]{1,0:T(8,128)(2,1)S(1)}, u32[]{:S(2)}, u32[]{:S(2)}) collective-permute-start(bf16[512,128]{1,0:T(8,128)(2,1)S(1)} %get-tuple-element.12.refs_0_), channel_id=1, source_target_pairs={{0,2},{2,0},{4,6},{6,4},{8,10},{10,8},{12,14},{14,12},{16,18},{18,... | collective-permute-start | bytes 393224 | tf_op jit(solution)/shard_map/ppermute | solution.py:41
  7.7 1.4 %collective-permute-start.13 = (bf16[512,128]{1,0:T(8,128)(2,1)S(1)}, bf16[512,128]{1,0:T(8,128)(2,1)S(1)}, u32[]{:S(2)}, u32[]{:S(2)}) collective-permute-start(bf16[512,128]{1,0:T(8,128)(2,1)S(1)} %get-tuple-element.15.refs_0_), channel_id=1, source_target_pairs={{0,10},{2,8},{4,14},{6,12},{8,2},{10,0},{12,6},{14,4},{16,26},{18,... | collective-permute-start | bytes 393224 | tf_op jit(solution)/shard_map/ppermute | solution.py:41
  9.1 0.2 collective-permute-start.11
  9.3 2.0 %collective-permute-start.9 = (bf16[512,128]{1,0:T(8,128)(2,1)S(1)}, bf16[512,128]{1,0:T(8,128)(2,1)S(1)}, u32[]{:S(2)}, u32[]{:S(2)}) collective-permute-start(bf16[512,128]{1,0:T(8,128)(2,1)S(1)} %get-tuple-element.15.refs_0_), channel_id=1, source_target_pairs={{0,8},{2,10},{4,12},{6,14},{8,0},{10,2},{12,4},{14,6},{16,24},{18,... | collective-permute-start | bytes 393224 | tf_op jit(solution)/shard_map/ppermute | solution.py:41
  11.2 2.4 %collective-permute-start.1 = (bf16[512,128]{1,0:T(8,128)(2,1)S(1)}, bf16[512,128]{1,0:T(8,128)(2,1)S(1)}, u32[]{:S(2)}, u32[]{:S(2)}) collective-permute-start(bf16[512,128]{1,0:T(8,128)(2,1)S(1)} %get-tuple-element.12.refs_0_), channel_id=1, source_target_pairs={{0,8},{2,10},{4,12},{6,14},{8,0},{10,2},{12,4},{14,6},{16,24},{18,... | collective-permute-start | bytes 393224 | tf_op jit(solution)/shard_map/ppermute | solution.py:41
  13.6 2.8 %collective-permute-done.3.refs_4_ = bf16[512,128]{1,0:T(8,128)(2,1)S(1)} collective-permute-done((bf16[512,128]{1,0:T(8,128)(2,1)S(1)}, bf16[512,128]{1,0:T(8,128)(2,1)S(1)}, u32[]{:S(2)}, u32[]{:S(2)}) %collective-permute-start.3) | collective-permute-done | bytes 131104 | tf_op jit(solution)/shard_map/ppermute | solution.py:41
  16.4 0.5 %collective-permute-start.14 = (bf16[512,128]{1,0:T(8,128)(2,1)S(1)}, bf16[512,128]{1,0:T(8,128)(2,1)S(1)}, u32[]{:S(2)}, u32[]{:S(2)}) collective-permute-start(bf16[512,128]{1,0:T(8,128)(2,1)S(1)} %collective-permute-done.13.refs_6_), channel_id=1, source_target_pairs={{0,4},{2,6},{4,0},{6,2},{8,12},{10,14},{12,8},{14,10},{16,20},{18,... | collective-permute-start | bytes 393224 | tf_op jit(solution)/shard_map/ppermute | solution.py:41
  16.9 2.2 %collective-permute-done.11.refs_4_ = bf16[512,128]{1,0:T(8,128)(2,1)S(1)} collective-permute-done((bf16[512,128]{1,0:T(8,128)(2,1)S(1)}, bf16[512,128]{1,0:T(8,128)(2,1)S(1)}, u32[]{:S(2)}, u32[]{:S(2)}) %collective-permute-start.11) | collective-permute-done | bytes 131104 | tf_op jit(solution)/shard_map/ppermute | solution.py:41
  19.1 0.5 %collective-permute-start.10 = (bf16[512,128]{1,0:T(8,128)(2,1)S(1)}, bf16[512,128]{1,0:T(8,128)(2,1)S(1)}, u32[]{:S(2)}, u32[]{:S(2)}) collective-permute-start(bf16[512,128]{1,0:T(8,128)(2,1)S(1)} %collective-permute-done.9.refs_2_), channel_id=1, source_target_pairs={{0,4},{2,6},{4,0},{6,2},{8,12},{10,14},{12,8},{14,10},{16,20},{18,... | collective-permute-start | bytes 393224 | tf_op jit(solution)/shard_map/ppermute | solution.py:41
  19.7 0.4 %collective-permute-start.6 = (bf16[512,128]{1,0:T(8,128)(2,1)S(1)}, bf16[512,128]{1,0:T(8,128)(2,1)S(1)}, u32[]{:S(2)}, u32[]{:S(2)}) collective-permute-start(bf16[512,128]{1,0:T(8,128)(2,1)S(1)} %collective-permute-done.5.refs_6_), channel_id=1, source_target_pairs={{0,4},{2,6},{4,0},{6,2},{8,12},{10,14},{12,8},{14,10},{16,20},{18,... | collective-permute-start | bytes 393224 | tf_op jit(solution)/shard_map/ppermute | solution.py:41
  20.2 0.2 collective-permute-done.12.refs_5_
  20.5 0.2 collective-permute-start.2
  20.7 1.3 %tables.1.refs_8_ = bf16[8,128,256]{2,1,0:T(8,128)(2,1)S(1)} custom-call(bf16[8,8,64,64]{3,2,1,0:T(8,128)(2,1)S(1)} %copy-done.3, bf16[2,2,64,64]{3,2,1,0:T(8,128)(2,1)S(1)} %copy-done.6, bf16[64,512]{1,0:T(8,128)(2,1)S(1)} %bitcast.13), custom_call_target="tpu_custom_call" | custom-call | flops 200000000 | bytes 2000000 | tf_op jit(solution)/shard_map/tables/pallas_call | solution.py:160
  22.0 0.4 %mix.3 = (bf16[512,128]{1,0:T(8,128)(2,1)S(1)}, f32[512,128]{1,0:T(8,128)S(1)}) custom-call(bf16[512,128]{1,0:T(8,128)(2,1)S(1)} %get-tuple-element.15.refs_0_, bf16[512,128]{1,0:T(8,128)(2,1)S(1)} %collective-permute-done.8.refs_1_, bf16[512,128]{1,0:T(8,128)(2,1)S(1)} %collective-permute-done.9.refs_2_, ...), custom_call_target="tpu_custom_call" | custom-call | flops 268435456 | bytes 1048576 | tf_op jit(solution)/shard_map/mix/pallas_call | solution.py:220
  22.5 2.8 %collective-permute-start.15 = (bf16[512,128]{1,0:T(8,128)(2,1)S(1)}, bf16[512,128]{1,0:T(8,128)(2,1)S(1)}, u32[]{:S(2)}, u32[]{:S(2)}) collective-permute-start(bf16[512,128]{1,0:T(8,128)(2,1)S(1)} %get-tuple-element.17), channel_id=1, source_target_pairs={{0,16},{2,18},{4,20},{6,22},{8,24},{10,26},{12,28},{14,30},{16,0},... | collective-permute-start | bytes 393224 | tf_op jit(solution)/shard_map/ppermute | solution.py:41
  25.3 0.4 %mix.2 = (bf16[512,128]{1,0:T(8,128)(2,1)S(1)}, f32[512,128]{1,0:T(8,128)S(1)}) custom-call(bf16[512,128]{1,0:T(8,128)(2,1)S(1)} %get-tuple-element.12.refs_0_, bf16[512,128]{1,0:T(8,128)(2,1)S(1)} %collective-permute-done.refs_1_, bf16[512,128]{1,0:T(8,128)(2,1)S(1)} %collective-permute-done.1.refs_2_, bf16[512,128]{1,0:T(8,128)(2,1)S(1)} %collective-permute-done.2.refs_3_, ...), custom_call_target="tpu_custom_call" | custom-call | flops 268435456 | bytes 1048576 | tf_op jit(solution)/shard_map/mix/pallas_call | solution.py:220
  25.7 0.3 collective-permute-start.7
  26.0 0.5 %threshold_map.1.refs_4_ = f32[128,512]{1,0:T(8,128)S(1)} custom-call(s32[128,256]{1,0:T(8,128)S(1)} %bitcast.16, f32[8,16]{1,0:T(8,128)S(1)} %copy-done.7), custom_call_target="tpu_custom_call" | custom-call | flops 2097152 | bytes 262144 | tf_op jit(solution)/shard_map/threshold_map/pallas_call | solution.py:194
  26.5 8.9 %collective-permute-done.15.refs_1_ = bf16[512,128]{1,0:T(8,128)(2,1)S(1)} collective-permute-done((bf16[512,128]{1,0:T(8,128)(2,1)S(1)}, bf16[512,128]{1,0:T(8,128)(2,1)S(1)}, u32[]{:S(2)}, u32[]{:S(2)}) %collective-permute-start.15) | collective-permute-done | bytes 131104 | tf_op jit(solution)/shard_map/ppermute | solution.py:41
  35.4 2.1 %finish.2 = (f32[1024,512]{1,0:T(8,128)}, bf16[1024,512]{1,0:T(8,128)(2,1)}) custom-call(f32[512,128]{1,0:T(8,128)S(1)} %get-tuple-element.16.refs_0_, bf16[512,128]{1,0:T(8,128)(2,1)S(1)} %collective-permute-done.15.refs_1_, bf16[1024,512]{1,0:T(8,128)(2,1)S(1)} %bitcast.7, bf16[1024,512]{1,0:T(8,128)(2,1)S(1)} %bitcast.10, ...), custom_call_target="tpu_custom_call" | custom-call | flops 134217728 | bytes 2621440 | tf_op jit(solution)/shard_map/finish/pallas_call | solution.py:263
  37.5 0.1 collective-permute-done.7.refs_1_
  37.6 2.1 %finish.3 = (f32[1024,512]{1,0:T(8,128)}, bf16[1024,512]{1,0:T(8,128)(2,1)}) custom-call(f32[512,128]{1,0:T(8,128)S(1)} %get-tuple-element.13.refs_0_, bf16[512,128]{1,0:T(8,128)(2,1)S(1)} %collective-permute-done.7.refs_1_, bf16[1024,512]{1,0:T(8,128)(2,1)S(1)} %bitcast.8, ...), custom_call_target="tpu_custom_call", output_to_operand_aliasing={{0}: (7, {}), {1}: (8, {})} | custom-call | flops 134217728 | bytes 2621440 | tf_op jit(solution)/shard_map/finish/pallas_call | solution.py:263
  (31 shorter events, 0.2 us)
Async XLA Ops:
  0.6 20.0 %copy-start.2 = (bf16[512,64]{0,1:T(8,128)(2,1)S(1)}, bf16[512,64]{0,1:T(8,128)(2,1)}, u32[]{:S(2)}) copy-start(bf16[512,64]{0,1:T(8,128)(2,1)} %param.12) | copy-start | bytes 196612
  0.6 20.0 %copy-start.6 = (bf16[2,2,64,64]{3,2,1,0:T(8,128)(2,1)S(1)}, bf16[2,2,64,64]{3,2,1,0:T(8,128)(2,1)}, u32[]{:S(2)}) copy-start(bf16[2,2,64,64]{3,2,1,0:T(8,128)(2,1)} %ty_ref.1) | copy-start | bytes 98308
  0.7 20.0 %copy-start.3 = (bf16[8,8,64,64]{3,2,1,0:T(8,128)(2,1)S(1)}, bf16[8,8,64,64]{3,2,1,0:T(8,128)(2,1)}, u32[]{:S(2)}) copy-start(bf16[8,8,64,64]{3,2,1,0:T(8,128)(2,1)} %tx_ref.1) | copy-start | bytes 1572868
  3.2 8.1 %collective-permute-start.5 = (bf16[512,128]{1,0:T(8,128)(2,1)S(1)}, bf16[512,128]{1,0:T(8,128)(2,1)S(1)}, u32[]{:S(2)}, u32[]{:S(2)}) collective-permute-start(bf16[512,128]{1,0:T(8,128)(2,1)S(1)} %get-tuple-element.12.refs_0_), channel_id=1, source_target_pairs={{0,10},{2,8},{4,14},{6,12},{8,2},{10,0},{12,6},{14,4},{16,26},{18,... | collective-permute-start | bytes 393224 | tf_op jit(solution)/shard_map/ppermute | solution.py:41
  7.2 9.2 %collective-permute-start.3 = (bf16[512,128]{1,0:T(8,128)(2,1)S(1)}, bf16[512,128]{1,0:T(8,128)(2,1)S(1)}, u32[]{:S(2)}, u32[]{:S(2)}) collective-permute-start(bf16[512,128]{1,0:T(8,128)(2,1)S(1)} %get-tuple-element.12.refs_0_), channel_id=1, source_target_pairs={{0,2},{2,0},{4,6},{6,4},{8,10},{10,8},{12,14},{14,12},{16,18},{18,... | collective-permute-start | bytes 393224 | tf_op jit(solution)/shard_map/ppermute | solution.py:41
  7.7 18.2 %copy-start.5 = (s32[8,16,256]{2,1,0:T(8,128)S(1)}, s32[8,16,256]{2,1,0:T(8,128)}, u32[]{:S(2)}) copy-start(s32[8,16,256]{2,1,0:T(8,128)} %param.11) | copy-start | bytes 393220
  7.7 18.2 %copy-start.7 = (f32[8,16]{1,0:T(8,128)S(1)}, f32[8,16]{1,0:T(8,128)}, u32[]{:S(2)}) copy-start(f32[8,16]{1,0:T(8,128)} %threshold_ref.1) | copy-start | bytes 1540
  7.7 8.7 %collective-permute-start.13 = (bf16[512,128]{1,0:T(8,128)(2,1)S(1)}, bf16[512,128]{1,0:T(8,128)(2,1)S(1)}, u32[]{:S(2)}, u32[]{:S(2)}) collective-permute-start(bf16[512,128]{1,0:T(8,128)(2,1)S(1)} %get-tuple-element.15.refs_0_), channel_id=1, source_target_pairs={{0,10},{2,8},{4,14},{6,12},{8,2},{10,0},{12,6},{14,4},{16,26},{18,... | collective-permute-start | bytes 393224 | tf_op jit(solution)/shard_map/ppermute | solution.py:41
  9.1 10.0 %collective-permute-start.11 = (bf16[512,128]{1,0:T(8,128)(2,1)S(1)}, bf16[512,128]{1,0:T(8,128)(2,1)S(1)}, u32[]{:S(2)}, u32[]{:S(2)}) collective-permute-start(bf16[512,128]{1,0:T(8,128)(2,1)S(1)} %get-tuple-element.15.refs_0_), channel_id=1, source_target_pairs={{0,2},{2,0},{4,6},{6,4},{8,10},{10,8},{12,14},{14,12},{16,18},{18,... | collective-permute-start | bytes 393224 | tf_op jit(solution)/shard_map/ppermute | solution.py:41
  9.3 9.9 %collective-permute-start.9 = (bf16[512,128]{1,0:T(8,128)(2,1)S(1)}, bf16[512,128]{1,0:T(8,128)(2,1)S(1)}, u32[]{:S(2)}, u32[]{:S(2)}) collective-permute-start(bf16[512,128]{1,0:T(8,128)(2,1)S(1)} %get-tuple-element.15.refs_0_), channel_id=1, source_target_pairs={{0,8},{2,10},{4,12},{6,14},{8,0},{10,2},{12,4},{14,6},{16,24},{18,... | collective-permute-start | bytes 393224 | tf_op jit(solution)/shard_map/ppermute | solution.py:41
  11.2 8.4 %collective-permute-start.1 = (bf16[512,128]{1,0:T(8,128)(2,1)S(1)}, bf16[512,128]{1,0:T(8,128)(2,1)S(1)}, u32[]{:S(2)}, u32[]{:S(2)}) collective-permute-start(bf16[512,128]{1,0:T(8,128)(2,1)S(1)} %get-tuple-element.12.refs_0_), channel_id=1, source_target_pairs={{0,8},{2,10},{4,12},{6,14},{8,0},{10,2},{12,4},{14,6},{16,24},{18,... | collective-permute-start | bytes 393224 | tf_op jit(solution)/shard_map/ppermute | solution.py:41
  16.4 3.3 %collective-permute-start.8 = (bf16[512,128]{1,0:T(8,128)(2,1)S(1)}, bf16[512,128]{1,0:T(8,128)(2,1)S(1)}, u32[]{:S(2)}, u32[]{:S(2)}) collective-permute-start(bf16[512,128]{1,0:T(8,128)(2,1)S(1)} %get-tuple-element.15.refs_0_), channel_id=1, source_target_pairs={{0,4},{2,6},{4,0},{6,2},{8,12},{10,14},{12,8},{14,10},{16,20},{18,... | collective-permute-start | bytes 393224 | tf_op jit(solution)/shard_map/ppermute | solution.py:41
  16.4 3.7 %collective-permute-start.14 = (bf16[512,128]{1,0:T(8,128)(2,1)S(1)}, bf16[512,128]{1,0:T(8,128)(2,1)S(1)}, u32[]{:S(2)}, u32[]{:S(2)}) collective-permute-start(bf16[512,128]{1,0:T(8,128)(2,1)S(1)} %collective-permute-done.13.refs_6_), channel_id=1, source_target_pairs={{0,4},{2,6},{4,0},{6,2},{8,12},{10,14},{12,8},{14,10},{16,20},{18,... | collective-permute-start | bytes 393224 | tf_op jit(solution)/shard_map/ppermute | solution.py:41
  19.1 1.3 %collective-permute-start.12 = (bf16[512,128]{1,0:T(8,128)(2,1)S(1)}, bf16[512,128]{1,0:T(8,128)(2,1)S(1)}, u32[]{:S(2)}, u32[]{:S(2)}) collective-permute-start(bf16[512,128]{1,0:T(8,128)(2,1)S(1)} %collective-permute-done.11.refs_4_), channel_id=1, source_target_pairs={{0,4},{2,6},{4,0},{6,2},{8,12},{10,14},{12,8},{14,10},{16,20},{18,... | collective-permute-start | bytes 393224 | tf_op jit(solution)/shard_map/ppermute | solution.py:41
  19.1 2.9 %collective-permute-start.10 = (bf16[512,128]{1,0:T(8,128)(2,1)S(1)}, bf16[512,128]{1,0:T(8,128)(2,1)S(1)}, u32[]{:S(2)}, u32[]{:S(2)}) collective-permute-start(bf16[512,128]{1,0:T(8,128)(2,1)S(1)} %collective-permute-done.9.refs_2_), channel_id=1, source_target_pairs={{0,4},{2,6},{4,0},{6,2},{8,12},{10,14},{12,8},{14,10},{16,20},{18,... | collective-permute-start | bytes 393224 | tf_op jit(solution)/shard_map/ppermute | solution.py:41
  19.6 5.6 %collective-permute-start = (bf16[512,128]{1,0:T(8,128)(2,1)S(1)}, bf16[512,128]{1,0:T(8,128)(2,1)S(1)}, u32[]{:S(2)}, u32[]{:S(2)}) collective-permute-start(bf16[512,128]{1,0:T(8,128)(2,1)S(1)} %get-tuple-element.12.refs_0_), channel_id=1, source_target_pairs={{0,4},{2,6},{4,0},{6,2},{8,12},{10,14},{12,8},{14,10},{16,20},{18,... | collective-permute-start | bytes 393224 | tf_op jit(solution)/shard_map/ppermute | solution.py:41
  19.7 5.5 %collective-permute-start.6 = (bf16[512,128]{1,0:T(8,128)(2,1)S(1)}, bf16[512,128]{1,0:T(8,128)(2,1)S(1)}, u32[]{:S(2)}, u32[]{:S(2)}) collective-permute-start(bf16[512,128]{1,0:T(8,128)(2,1)S(1)} %collective-permute-done.5.refs_6_), channel_id=1, source_target_pairs={{0,4},{2,6},{4,0},{6,2},{8,12},{10,14},{12,8},{14,10},{16,20},{18,... | collective-permute-start | bytes 393224 | tf_op jit(solution)/shard_map/ppermute | solution.py:41
  20.2 5.1 %collective-permute-start.4 = (bf16[512,128]{1,0:T(8,128)(2,1)S(1)}, bf16[512,128]{1,0:T(8,128)(2,1)S(1)}, u32[]{:S(2)}, u32[]{:S(2)}) collective-permute-start(bf16[512,128]{1,0:T(8,128)(2,1)S(1)} %collective-permute-done.3.refs_4_), channel_id=1, source_target_pairs={{0,4},{2,6},{4,0},{6,2},{8,12},{10,14},{12,8},{14,10},{16,20},{18,... | collective-permute-start | bytes 393224 | tf_op jit(solution)/shard_map/ppermute | solution.py:41
  20.5 4.8 %collective-permute-start.2 = (bf16[512,128]{1,0:T(8,128)(2,1)S(1)}, bf16[512,128]{1,0:T(8,128)(2,1)S(1)}, u32[]{:S(2)}, u32[]{:S(2)}) collective-permute-start(bf16[512,128]{1,0:T(8,128)(2,1)S(1)} %collective-permute-done.1.refs_2_), channel_id=1, source_target_pairs={{0,4},{2,6},{4,0},{6,2},{8,12},{10,14},{12,8},{14,10},{16,20},{18,... | collective-permute-start | bytes 393224 | tf_op jit(solution)/shard_map/ppermute | solution.py:41
  22.0 13.4 %copy-start = (bf16[8,8,16,512]{3,2,1,0:T(8,128)(2,1)S(1)}, bf16[8,8,16,512]{3,2,1,0:T(8,128)(2,1)}, u32[]{:S(2)}) copy-start(bf16[8,8,16,512]{3,2,1,0:T(8,128)(2,1)} %param.9) | copy-start | bytes 3145732
  22.0 13.4 %copy-start.1 = (bf16[8,8,16,512]{3,2,1,0:T(8,128)(2,1)S(1)}, bf16[8,8,16,512]{3,2,1,0:T(8,128)(2,1)}, u32[]{:S(2)}) copy-start(bf16[8,8,16,512]{3,2,1,0:T(8,128)(2,1)} %param.8) | copy-start | bytes 3145732
  22.0 13.4 %copy-start.4 = (bf16[64,512]{1,0:T(8,128)(2,1)S(1)}, bf16[64,512]{1,0:T(8,128)(2,1)}, u32[]{:S(2)}) copy-start(bf16[64,512]{1,0:T(8,128)(2,1)} %refs_5_.3) | copy-start | bytes 196612
  22.5 13.0 %collective-permute-start.15 = (bf16[512,128]{1,0:T(8,128)(2,1)S(1)}, bf16[512,128]{1,0:T(8,128)(2,1)S(1)}, u32[]{:S(2)}, u32[]{:S(2)}) collective-permute-start(bf16[512,128]{1,0:T(8,128)(2,1)S(1)} %get-tuple-element.17), channel_id=1, source_target_pairs={{0,16},{2,18},{4,20},{6,22},{8,24},{10,26},{12,28},{14,30},{16,0},... | collective-permute-start | bytes 393224 | tf_op jit(solution)/shard_map/ppermute | solution.py:41
  25.7 11.9 %collective-permute-start.7 = (bf16[512,128]{1,0:T(8,128)(2,1)S(1)}, bf16[512,128]{1,0:T(8,128)(2,1)S(1)}, u32[]{:S(2)}, u32[]{:S(2)}) collective-permute-start(bf16[512,128]{1,0:T(8,128)(2,1)S(1)} %get-tuple-element.14), channel_id=1, source_target_pairs={{0,16},{2,18},{4,20},{6,22},{8,24},{10,26},{12,28},{14,30},{16,0},... | collective-permute-start | bytes 393224 | tf_op jit(solution)/shard_map/ppermute | solution.py:41
where the time goes:
time: 39.9 us; the launch traced here: 39.7 us
  starting transfers between devices  15.3 us (38%)
  waiting for transfers between devices  14.2 us (36%)
  Pallas kernels  9.37 us (23%)
  between operations  0.75 us (2%)
    ppermute x16, starting transfers between devices, swap(): return lax.ppermute(x, axes, pairs)  15.3 us
    ppermute x16, waiting for transfers between devices, swap(): return lax.ppermute(x, axes, pairs)  14.2 us
    pallas_call x2, Pallas kernels, finish(): pl.pallas_call(functools.partial(finish_kernel, first), grid=(rows // blo...  4.23 us
    pallas_call x1, Pallas kernels, coefficients(): pl.pallas_call(coeff_kernel, in_specs=[ANY] * 4, out_specs=[VMEM] * chunk...  2.48 us
    pallas_call x1, Pallas kernels, make_tables(): pl.pallas_call(functools.partial(table_kernel, n_gy, near), in_specs=[VME...  1.28 us
    pallas_call x2, Pallas kernels, mix(): pl.pallas_call(functools.partial(mix_kernel, count), in_specs=[VMEM] * (c...  0.87 us
  transfers between devices with their start and end apart: 16, of which 5 were waited for; matrix products, arithmetic and copies ran while one was open for 0% of the time, Pallas kernels for 12%

commit v1 on v0

v1 whole, which is shorter than its diff:
```python
import functools

import jax
import jax.numpy as jnp
from jax import lax
from jax.experimental import pallas as pl
from jax.experimental.pallas import tpu as pltpu
from jax.sharding import PartitionSpec as P


SIZES = (1, 1)
F32 = jnp.float32
BF16 = jnp.bfloat16


def mm(a, b):
    return lax.dot_general(a, b, (((1,), (0,)), ((), ())), preferred_element_type=F32)


def mm_nt(a, b):
    return lax.dot_general(a, b, (((1,), (1,)), ((), ())), preferred_element_type=F32)


def swap(x, axes, mesh_shape, masks):
    sizes = [mesh_shape[axis] for axis in axes]
    total = 1
    for size in sizes:
        total *= size
    pairs = []
    for source in range(total):
        rest, coords = source, []
        for size in reversed(sizes):
            coords.append(rest % size)
            rest //= size
        coords.reverse()
        target = 0
        for coord, mask, size in zip(coords, masks, sizes):
            target = target * size + (coord ^ mask)
        pairs.append((source, target))
    return lax.ppermute(x, axes, pairs)


VMEM = pl.BlockSpec(memory_space=pltpu.VMEM)
ANY = pl.BlockSpec(memory_space=pl.ANY)
PARAMS = pltpu.CompilerParams(vmem_limit_bytes=8 << 20)


def split(gathers):
    parts = sum(SIZES)
    return [gathers * part // parts for part in SIZES] if gathers % parts == 0 else [gathers]


def coeff_kernel(count, *refs):
    model_hbm, samples_hbm, eval_hbm, basis_hbm = refs[:4]
    outs = refs[4 : 4 + count]
    model_ref, samples_ref, weight_ref, sems = refs[4 + count :]
    k = eval_hbm.shape[0]
    copies = [
        pltpu.make_async_copy(eval_hbm, weight_ref.at[pl.ds(0, k)], sems.at[0]),
        pltpu.make_async_copy(basis_hbm, weight_ref.at[pl.ds(k, k)], sems.at[1]),
    ]
    first = 0
    for i, out_ref in enumerate(outs):
        part = pl.ds(first, out_ref.shape[0])
        first += out_ref.shape[0]
        copies.append(pltpu.make_async_copy(model_hbm.at[part], model_ref.at[part], sems.at[2 + 2 * i]))
        copies.append(pltpu.make_async_copy(samples_hbm.at[part], samples_ref.at[part], sems.at[3 + 2 * i]))
    for copy in copies:
        copy.start()
    copies[0].wait()
    copies[1].wait()
    weights = weight_ref[...].T
    first = 0
    for i, out_ref in enumerate(outs):
        rows = out_ref.shape[0]
        part = pl.ds(first, rows)
        first += rows
        copies[2 + 2 * i].wait()
        copies[3 + 2 * i].wait()
        top = mm(model_ref[part], weights)
        low = mm(samples_ref[part], weights)
        lane = lax.broadcasted_iota(jnp.int32, (rows, 2 * k), 1)
        out_ref[...] = jnp.where(lane < k, top, low).astype(BF16)


def coefficients(model, samples, evals, basis_t, counts):
    rows, width = model.shape
    k = evals.shape[0]
    return pl.pallas_call(
        functools.partial(coeff_kernel, len(counts)),
        in_specs=[ANY] * 4,
        out_specs=[VMEM] * len(counts),
        out_shape=[pltpu.VMEM((count, 2 * k), BF16) for count in counts],
        scratch_shapes=[
            pltpu.VMEM((rows, width), BF16),
            pltpu.VMEM((rows, width), BF16),
            pltpu.VMEM((2 * k, width), BF16),
            pltpu.SemaphoreType.DMA((2 + 2 * len(counts),)),
        ],
        cost_estimate=pl.CostEstimate(
            flops=8 * rows * width * k, bytes_accessed=4 * rows * (width + k), transcendentals=0
        ),
        name="coefficients",
    )(model, samples, evals, basis_t)


def diagonal(block, count):
    zero = jnp.zeros_like(block)
    rows = [jnp.concatenate([block if i == j else zero for j in range(count)], axis=1) for i in range(count)]
    return jnp.concatenate(rows, axis=0)


def table_kernel(n_gy, near, tx_ref, ty_ref, basis_ref, gather_ref, scatter_ref):
    k = basis_ref.shape[0]
    own_x, own_y = lax.axis_index("gx"), lax.axis_index("gy")
    flat = tx_ref.shape[1] * k
    masks = sorted({*range(near), near, near + 1})
    turned = {m: tx_ref[own_x ^ m].reshape(flat, k).T for m in masks}
    span = 4
    stacked = jnp.concatenate([basis_ref[...]] * span, axis=0)
    gram = mm_nt(stacked, stacked)
    row = lax.broadcasted_iota(jnp.int32, gram.shape, 0) // k
    col = lax.broadcasted_iota(jnp.int32, gram.shape, 1) // k
    gram = jnp.where(row == col, gram, 0.0).astype(BF16)
    lane = lax.broadcasted_iota(jnp.int32, (k, 2 * k), 1)

    def crossed(sources, targets):
        ends = jnp.concatenate([turned[m] for m in targets], axis=0)
        step = span * k
        ends = jnp.concatenate(
            [mm(ends[:, i : i + step], gram).astype(BF16) for i in range(0, flat, step)], axis=1
        )
        return mm_nt(jnp.concatenate([turned[m] for m in sources], axis=0), ends).astype(BF16)

    def store(out_ref, slot, where, i, forward, normal, back):
        here = slice(i // 2 * 2 * k, i // 2 * 2 * k + 2 * k)
        forward, normal = forward[:, here], normal[:, here]
        if i % 2:
            forward = jnp.roll(forward, k, axis=1)
        else:
            normal = jnp.roll(normal, k, axis=1)
        lanes = slice(where * 2 * k, (where + 1) * 2 * k)
        out_ref[slot, :k, lanes] = jnp.where(lane < k, forward, -normal).astype(BF16)
        out_ref[slot, k:, lanes] = jnp.where(lane < k, 0.0, back).astype(BF16)

    targets = (0, near)
    cross = crossed(range(near), targets)
    y_turned = [ty_ref[s].reshape(n_gy * k, k).T for s in range(n_gy)]
    inner = [mm(cross, diagonal(ty_ref[own_y, m], 2)).astype(BF16) for m in range(n_gy)]
    for m in range(near):
        source = own_x ^ m
        parts = jnp.concatenate([part[m * k : (m + 1) * k] for part in inner], axis=0)
        to_rows = jnp.concatenate([tx_ref[source, own_x ^ t] for t in targets], axis=0)
        from_rows = jnp.concatenate([tx_ref[own_x ^ t, source] for t in targets], axis=0)
        for s in range(n_gy):
            normal = mm(y_turned[s], parts)
            forward = mm_nt(ty_ref[s, own_y].T, to_rows)
            back = mm(from_rows, jnp.concatenate([ty_ref[own_y, s]] * 2, axis=1))
            for i in range(2):
                store(gather_ref, (s ^ own_y) * near + m, i, i, forward, normal, back[i * k : (i + 1) * k])

    sources = (0, 1, near, near + 1)
    targets = range(0, near, 2)
    count = len(targets)
    cross = crossed(sources, targets)
    own_turned = ty_ref[own_y].reshape(n_gy * k, k).T
    for my in range(n_gy):
        target_y = own_y ^ my
        inner = [mm(cross, diagonal(ty_ref[target_y, m], count)).astype(BF16) for m in range(n_gy)]
        y_forward = ty_ref[own_y, target_y].T
        y_back = jnp.concatenate([ty_ref[target_y, own_y]] * 2, axis=1)
        for n, m in enumerate(sources):
            source = own_x ^ m
            parts = jnp.concatenate([part[n * k : (n + 1) * k] for part in inner], axis=0)
            normal = mm(own_turned, parts)
            forward = mm_nt(y_forward, jnp.concatenate([tx_ref[source, own_x ^ t] for t in targets], axis=0))
            back = mm(jnp.concatenate([tx_ref[own_x ^ t, source] for t in targets], axis=0), y_back)
            for i in range(count):
                store(scatter_ref, n, my * count + i, i, forward, normal, back[i * k : (i + 1) * k])


def make_tables(n_gy, near, transfer_x, transfer_y, basis_t):
    k = transfer_x.shape[3]
    return pl.pallas_call(
        functools.partial(table_kernel, n_gy, near),
        in_specs=[VMEM] * 3,
        out_specs=[VMEM] * 2,
        out_shape=[
            jax.ShapeDtypeStruct((n_gy * near, 2 * k, 4 * k), BF16),
            jax.ShapeDtypeStruct((4, 2 * k, n_gy * near * k), BF16),
        ],
        cost_estimate=pl.CostEstimate(
            flops=200000000, bytes_accessed=2000000, transcendentals=0
        ),
        compiler_params=PARAMS,
        name="tables",
    )(transfer_x, transfer_y, basis_t)


def mask_kernel(support_ref, threshold_ref, out_ref):
    count = out_ref.shape[1]
    picked = support_ref[...].T
    word, bit = picked >> 5, jnp.int32(1) << (picked & 31)
    words = count // 32
    index = lax.broadcasted_iota(jnp.int32, (words, picked.shape[1]), 0)
    bits = jnp.zeros(index.shape, jnp.int32)
    for j in range(picked.shape[0]):
        bits = bits | jnp.where(index == word[j : j + 1], bit[j : j + 1], 0)
    shift = lax.broadcasted_iota(jnp.int32, (32, picked.shape[1]), 0)
    flags = jnp.concatenate([(bits[w : w + 1] >> shift) & 1 for w in range(words)], axis=0)
    kept = flags.T != 0
    levels = threshold_ref[...].T
    ly = levels.shape[0]
    for i in range(levels.shape[1]):
        rows = slice(i * ly, (i + 1) * ly)
        out_ref[rows] = jnp.where(kept[rows], levels[:, i : i + 1], jnp.inf)


def threshold_map(support, threshold, width):
    boxes = support.shape[0]
    return pl.pallas_call(
        mask_kernel,
        in_specs=[VMEM] * 2,
        out_specs=VMEM,
        out_shape=jax.ShapeDtypeStruct((boxes, width), F32),
        cost_estimate=pl.CostEstimate(
            flops=boxes * width * 32, bytes_accessed=4 * boxes * width, transcendentals=0
        ),
        compiler_params=PARAMS,
        name="threshold_map",
    )(support, threshold)


def mix_kernel(count, *refs):
    tables_ref, own_ref = refs[count : count + 2]
    sent = refs[count + 2 :]
    k2 = refs[0].shape[1]
    rows = refs[0].shape[0]
    tables = tables_ref[...].reshape(count * k2, tables_ref.shape[2])
    for i in range(0, rows, 256):
        here = slice(i, min(i + 256, rows))
        mixed = mm(jnp.concatenate([ref[here] for ref in refs[:count]], axis=1), tables)
        own_ref[here] = mixed[:, :k2]
        for j, out_ref in enumerate(sent):
            out_ref[here] = mixed[:, (j + 1) * k2 : (j + 2) * k2].astype(BF16)


def mix(parts, tables):
    rows, k2 = parts[0].shape
    count = len(parts)
    others = tables.shape[2] // k2 - 1
    return pl.pallas_call(
        functools.partial(mix_kernel, count),
        in_specs=[VMEM] * (count + 1),
        out_specs=[VMEM] * (1 + others),
        out_shape=[pltpu.VMEM((rows, k2), F32)] + [pltpu.VMEM((rows, k2), BF16)] * others,
        cost_estimate=pl.CostEstimate(
            flops=2 * rows * count * k2 * tables.shape[2],
            bytes_accessed=2 * rows * k2 * (count + others),
            transcendentals=0,
        ),
        compiler_params=PARAMS,
        name="mix",
    )(*parts, tables)


def finish_kernel(first, count, *refs):
    own_ref, arrived = refs[0], refs[1 : 1 + count]
    model_ref, samples_ref, limit_ref, eval_ref, basis_ref = refs[1 + count : 6 + count]
    next_hbm, residual_hbm, next_ref, residual_ref, sems = refs[-5:]
    zero = jnp.zeros(eval_ref.shape, BF16)
    to_data = jnp.concatenate([basis_ref[...], zero], axis=0)
    to_model = jnp.concatenate([zero, eval_ref[...]], axis=0)
    limit = limit_ref[...]
    boxes = limit.shape[0]
    copies = []
    for i in range(next_ref.shape[0]):
        rows, whole = pl.ds(i * boxes, boxes), pl.ds(first + i * boxes, boxes)
        both = own_ref[rows]
        for ref in arrived:
            both = both + ref[rows].astype(F32)
        both = both.astype(BF16)
        predicted = mm(both, to_data)
        residual_ref[i] = (samples_ref[whole].astype(F32) - predicted).astype(BF16)
        copies.append(pltpu.make_async_copy(residual_ref.at[i], residual_hbm.at[whole], sems.at[2 * i]))
        copies[-1].start()
        stepped = model_ref[whole].astype(F32) + mm(both, to_model)
        next_ref[i] = stepped - jnp.minimum(jnp.maximum(stepped, -limit), limit)
        copies.append(pltpu.make_async_copy(next_ref.at[i], next_hbm.at[whole], sems.at[2 * i + 1]))
        copies[-1].start()
    for copy in copies:
        copy.wait()


def finish(own, arrived, model, samples, limit, evals, basis_t, first, earlier):
    total, width = model.shape
    rows, k2 = own.shape
    boxes = limit.shape[0]
    pieces = rows // boxes
    return pl.pallas_call(
        functools.partial(finish_kernel, first, len(arrived)),
        in_specs=[VMEM] * (6 + len(arrived)) + [ANY] * len(earlier),
        out_specs=[ANY, ANY],
        out_shape=[
            jax.ShapeDtypeStruct((total, width), F32),
            jax.ShapeDtypeStruct((total, width), BF16),
        ],
        scratch_shapes=[
            pltpu.VMEM((pieces, boxes, width), F32),
            pltpu.VMEM((pieces, boxes, width), BF16),
            pltpu.SemaphoreType.DMA((2 * pieces,)),
        ],
        input_output_aliases={6 + len(arrived) + i: i for i in range(len(earlier))},
        cost_estimate=pl.CostEstimate(
            flops=4 * rows * width * k2, bytes_accessed=10 * rows * width, transcendentals=0
        ),
        compiler_params=PARAMS,
        name="finish",
    )(own, *arrived, model, samples, limit, evals, basis_t, *earlier)


def on_device(mesh_shape, samples, model_prev, threshold, support, sample_basis, eval_basis, transfer_x, transfer_y):
    n_gx, n_gy = mesh_shape["gx"], mesh_shape["gy"]
    near = n_gx // 2
    gathers, lx, ly, width = model_prev.shape
    boxes = lx * ly
    rows = gathers * boxes
    basis_t = sample_basis.T
    model = model_prev.reshape(rows, width)
    data = samples.reshape(rows, width)
    counts = [count * boxes for count in split(gathers)]
    firsts = [sum(counts[:c]) for c in range(len(counts))]
    axes = ("gx", "gy")

    def exchange(x, mx, my):
        return swap(x, axes, mesh_shape, (mx, my))

    around = [(mx, my) for my in range(n_gy) for mx in range(0, near, 2)]
    first, second = coefficients(model, data, eval_basis, basis_t, counts)
    gather, scatter = make_tables(n_gy, near, transfer_x, transfer_y, basis_t)
    limit = threshold_map(
        support.reshape(boxes, support.shape[2]), threshold, width
    )

    parts = []
    for mx, my in around:
        part = exchange(first, mx, my) if mx or my else first
        parts += [part, exchange(part, 1, 0)]
    own_first, far = mix(parts, gather)
    far_first = exchange(far, near, 0)

    far = exchange(second, near, 0)
    parts = [second, exchange(second, 1, 0), far, exchange(far, 1, 0)]
    own_second, *sent = mix(parts, scatter)
    arrived = [exchange(x, mx, my) for x, (mx, my) in zip(sent, around[1:])]

    outs = ()
    outs = finish(own_second, arrived, model, data, limit, eval_basis, basis_t, firsts[1], outs)
    outs = finish(own_first, [far_first], model, data, limit, eval_basis, basis_t, firsts[0], outs)
    model_next, residual = outs
    return model_next.reshape(model_prev.shape), residual.reshape(samples.shape)


def step(mesh_shape, *args):
    return on_device(mesh_shape, *args)


def solution(mesh):
    return jax.shard_map(
        functools.partial(step, dict(mesh.shape)),
        mesh=mesh,
        in_specs=(
            P("ga", "gx", "gy", None),
            P("ga", "gx", "gy", None),
            P("gx", "gy"),
            P("gx", "gy", None),
            P(),
            P(),
            P(),
            P(),
        ),
        out_specs=(P("ga", "gx", "gy", None), P("ga", "gx", "gy", None)),
        check_vma=False,
    )
```

time: 39.9 us -> 35.5 us (0.89)
  starting transfers between devices: 15.3 us -> 12.9 us
  waiting for transfers between devices: 14.2 us -> 13 us
  Pallas kernels: 9.37 us -> 8.68 us
    ppermute x16 -> x14, starting transfers between devices: 15.3 us -> 12.9 us  [swap(): return lax.ppermute(x, axes, pairs)]
    pallas_call x3, Pallas kernels: 6.71 us -> 5.07 us  [the longest x2 2.8 us: finish(): pl.pallas_call(functools.partial(finish_kernel, first, len(arrived)), in_...]
    ppermute x16 -> x14, waiting for transfers between devices: 14.2 us -> 13 us  [swap(): return lax.ppermute(x, axes, pairs)]
    pallas_call x1, Pallas kernels: 1.28 us -> 2.23 us  [make_tables(): pl.pallas_call(functools.partial(table_kernel, n_gy, near), in_specs=[VME...]
  transfers between devices with their start and end apart: 16 -> 14, of which waited for: 5 -> 8; matrix products, arithmetic and copies ran while one was open for 0% -> 0% of each run, Pallas kernels for 12% -> 14%
where the time goes in v1:
time: 35.5 us; the launch traced here: 35.4 us
  waiting for transfers between devices  13 us (37%)
  starting transfers between devices  12.9 us (36%)
  Pallas kernels  8.68 us (24%)
  between operations  0.76 us (2%)
    ppermute x14, waiting for transfers between devices, swap(): return lax.ppermute(x, axes, pairs)  13 us
    ppermute x14, starting transfers between devices, swap(): return lax.ppermute(x, axes, pairs)  12.9 us
    pallas_call x2, Pallas kernels, finish(): pl.pallas_call(functools.partial(finish_kernel, first, len(arrived)), in_...  2.8 us
    pallas_call x1, Pallas kernels, coefficients(): pl.pallas_call(functools.partial(coeff_kernel, len(counts)), in_specs=[AN...  2.27 us
    pallas_call x1, Pallas kernels, make_tables(): pl.pallas_call(functools.partial(table_kernel, n_gy, near), in_specs=[VME...  2.23 us
    pallas_call x2, Pallas kernels, mix(): pl.pallas_call(functools.partial(mix_kernel, count), in_specs=[VMEM] * (c...  0.87 us
  transfers between devices with their start and end apart: 14, of which 8 were waited for; matrix products, arithmetic and copies ran while one was open for 0% of the time, Pallas kernels for 14%

profile of v1, /device:TPU:0, one launch (start us, length us, event | category | flops | bytes accessed | tf_op | source)
XLA Modules:
  0.0 35.4 jit_solution(14446578773988283419)
XLA Ops:
  0.7 2.3 %coefficients.1 = (bf16[512,128]{1,0:T(8,128)(2,1)S(1)}, bf16[512,128]{1,0:T(8,128)(2,1)S(1)}) custom-call(bf16[1024,512]{1,0:T(8,128)(2,1)} %bitcast.6, bf16[1024,512]{1,0:T(8,128)(2,1)} %bitcast.9, bf16[64,512]{1,0:T(8,128)(2,1)} %refs_5_.1, bf16[64,512]{1,0:T(8,128)(2,1)} %bitcast.12), custom_call_target="tpu_custom_call" | custom-call | flops 268435456 | bytes 2359296 | tf_op jit(solution)/shard_map/coefficients/pallas_call | solution.py:89
  3.0 4.1 %collective-permute-start.9 = (bf16[512,128]{1,0:T(8,128)(2,1)S(1)}, bf16[512,128]{1,0:T(8,128)(2,1)S(1)}, u32[]{:S(2)}, u32[]{:S(2)}) collective-permute-start(bf16[512,128]{1,0:T(8,128)(2,1)S(1)} %get-tuple-element.20.refs_0_), channel_id=1, source_target_pairs={{0,16},{2,18},{4,20},{6,22},{8,24},{10,26},{12,28},{14,30},{16,0},... | collective-permute-start | bytes 393224 | tf_op jit(solution)/shard_map/ppermute | solution.py:40
  7.1 2.6 %collective-permute-start.5 = (bf16[512,128]{1,0:T(8,128)(2,1)S(1)}, bf16[512,128]{1,0:T(8,128)(2,1)S(1)}, u32[]{:S(2)}, u32[]{:S(2)}) collective-permute-start(bf16[512,128]{1,0:T(8,128)(2,1)S(1)} %get-tuple-element.16.refs_0_), channel_id=1, source_target_pairs={{0,10},{2,8},{4,14},{6,12},{8,2},{10,0},{12,6},{14,4},{16,26},{18,... | collective-permute-start | bytes 393224 | tf_op jit(solution)/shard_map/ppermute | solution.py:40
  9.7 0.6 %collective-permute-start.3 = (bf16[512,128]{1,0:T(8,128)(2,1)S(1)}, bf16[512,128]{1,0:T(8,128)(2,1)S(1)}, u32[]{:S(2)}, u32[]{:S(2)}) collective-permute-start(bf16[512,128]{1,0:T(8,128)(2,1)S(1)} %get-tuple-element.16.refs_0_), channel_id=1, source_target_pairs={{0,2},{2,0},{4,6},{6,4},{8,10},{10,8},{12,14},{14,12},{16,18},{18,... | collective-permute-start | bytes 393224 | tf_op jit(solution)/shard_map/ppermute | solution.py:40
  10.2 0.4 %collective-permute-start.1 = (bf16[512,128]{1,0:T(8,128)(2,1)S(1)}, bf16[512,128]{1,0:T(8,128)(2,1)S(1)}, u32[]{:S(2)}, u32[]{:S(2)}) collective-permute-start(bf16[512,128]{1,0:T(8,128)(2,1)S(1)} %get-tuple-element.16.refs_0_), channel_id=1, source_target_pairs={{0,8},{2,10},{4,12},{6,14},{8,0},{10,2},{12,4},{14,6},{16,24},{18,... | collective-permute-start | bytes 393224 | tf_op jit(solution)/shard_map/ppermute | solution.py:40
  10.7 2.9 %collective-permute-done.9.refs_2_ = bf16[512,128]{1,0:T(8,128)(2,1)S(1)} collective-permute-done((bf16[512,128]{1,0:T(8,128)(2,1)S(1)}, bf16[512,128]{1,0:T(8,128)(2,1)S(1)}, u32[]{:S(2)}, u32[]{:S(2)}) %collective-permute-start.9) | collective-permute-done | bytes 131104 | tf_op jit(solution)/shard_map/ppermute | solution.py:40
  13.5 0.5 %collective-permute-start = (bf16[512,128]{1,0:T(8,128)(2,1)S(1)}, bf16[512,128]{1,0:T(8,128)(2,1)S(1)}, u32[]{:S(2)}, u32[]{:S(2)}) collective-permute-start(bf16[512,128]{1,0:T(8,128)(2,1)S(1)} %get-tuple-element.16.refs_0_), channel_id=1, source_target_pairs={{0,4},{2,6},{4,0},{6,2},{8,12},{10,14},{12,8},{14,10},{16,20},{18,... | collective-permute-start | bytes 393224 | tf_op jit(solution)/shard_map/ppermute | solution.py:40
  14.0 2.1 %collective-permute-done.5.refs_6_ = bf16[512,128]{1,0:T(8,128)(2,1)S(1)} collective-permute-done((bf16[512,128]{1,0:T(8,128)(2,1)S(1)}, bf16[512,128]{1,0:T(8,128)(2,1)S(1)}, u32[]{:S(2)}, u32[]{:S(2)}) %collective-permute-start.5) | collective-permute-done | bytes 131104 | tf_op jit(solution)/shard_map/ppermute | solution.py:40
  16.1 1.0 %collective-permute-done.3.refs_4_ = bf16[512,128]{1,0:T(8,128)(2,1)S(1)} collective-permute-done((bf16[512,128]{1,0:T(8,128)(2,1)S(1)}, bf16[512,128]{1,0:T(8,128)(2,1)S(1)}, u32[]{:S(2)}, u32[]{:S(2)}) %collective-permute-start.3) | collective-permute-done | bytes 131104 | tf_op jit(solution)/shard_map/ppermute | solution.py:40
  17.1 1.3 %collective-permute-done.1.refs_2_ = bf16[512,128]{1,0:T(8,128)(2,1)S(1)} collective-permute-done((bf16[512,128]{1,0:T(8,128)(2,1)S(1)}, bf16[512,128]{1,0:T(8,128)(2,1)S(1)}, u32[]{:S(2)}, u32[]{:S(2)}) %collective-permute-start.1) | collective-permute-done | bytes 131104 | tf_op jit(solution)/shard_map/ppermute | solution.py:40
  18.4 2.2 %tables.1 = (bf16[8,128,256]{2,1,0:T(8,128)(2,1)S(1)}, bf16[4,128,512]{2,1,0:T(8,128)(2,1)S(1)}) custom-call(bf16[8,8,64,64]{3,2,1,0:T(8,128)(2,1)S(1)} %copy-done.3, bf16[2,2,64,64]{3,2,1,0:T(8,128)(2,1)S(1)} %copy-done.6, bf16[64,512]{1,0:T(8,128)(2,1)S(1)} %bitcast.13), custom_call_target="tpu_custom_call" | custom-call | flops 200000000 | bytes 2000000 | tf_op jit(solution)/shard_map/tables/pallas_call | solution.py:184
  20.7 0.4 %mix.3 = (f32[512,128]{1,0:T(8,128)S(1)}, bf16[512,128]{1,0:T(8,128)(2,1)S(1)}, bf16[512,128]{1,0:T(8,128)(2,1)S(1)}, bf16[512,128]{1,0:T(8,128)(2,1)S(1)}) custom-call(bf16[512,128]{1,0:T(8,128)(2,1)S(1)} %get-tuple-element.20.refs_0_, bf16[512,128]{1,0:T(8,128)(2,1)S(1)} %collective-permute-done.8.refs_1_, ...), custom_call_target="tpu_custom_call" | custom-call | flops 268435456 | bytes 917504 | tf_op jit(solution)/shard_map/mix/pallas_call | solution.py:252
  21.1 0.6 %collective-permute-start.11 = (bf16[512,128]{1,0:T(8,128)(2,1)S(1)}, bf16[512,128]{1,0:T(8,128)(2,1)S(1)}, u32[]{:S(2)}, u32[]{:S(2)}) collective-permute-start(bf16[512,128]{1,0:T(8,128)(2,1)S(1)} %get-tuple-element.23), channel_id=1, source_target_pairs={{0,8},{2,10},{4,12},{6,14},{8,0},{10,2},{12,4},{14,6},{16,24},{18,... | collective-permute-start | bytes 393224 | tf_op jit(solution)/shard_map/ppermute | solution.py:40
  21.7 0.6 %collective-permute-start.12 = (bf16[512,128]{1,0:T(8,128)(2,1)S(1)}, bf16[512,128]{1,0:T(8,128)(2,1)S(1)}, u32[]{:S(2)}, u32[]{:S(2)}) collective-permute-start(bf16[512,128]{1,0:T(8,128)(2,1)S(1)} %get-tuple-element.24), channel_id=1, source_target_pairs={{0,2},{2,0},{4,6},{6,4},{8,10},{10,8},{12,14},{14,12},{16,18},{18,... | collective-permute-start | bytes 393224 | tf_op jit(solution)/shard_map/ppermute | solution.py:40
  22.3 2.4 %collective-permute-start.13 = (bf16[512,128]{1,0:T(8,128)(2,1)S(1)}, bf16[512,128]{1,0:T(8,128)(2,1)S(1)}, u32[]{:S(2)}, u32[]{:S(2)}) collective-permute-start(bf16[512,128]{1,0:T(8,128)(2,1)S(1)} %get-tuple-element.25), channel_id=1, source_target_pairs={{0,10},{2,8},{4,14},{6,12},{8,2},{10,0},{12,6},{14,4},{16,26},{18,... | collective-permute-start | bytes 393224 | tf_op jit(solution)/shard_map/ppermute | solution.py:40
  24.7 0.4 %mix.2 = (f32[512,128]{1,0:T(8,128)S(1)}, bf16[512,128]{1,0:T(8,128)(2,1)S(1)}) custom-call(bf16[512,128]{1,0:T(8,128)(2,1)S(1)} %get-tuple-element.16.refs_0_, bf16[512,128]{1,0:T(8,128)(2,1)S(1)} %collective-permute-done.refs_1_, bf16[512,128]{1,0:T(8,128)(2,1)S(1)} %collective-permute-done.1.refs_2_, bf16[512,128]{1,0:T(8,128)(2,1)S(1)} %collective-permute-done.2.refs_3_, ...), custom_call_target="tpu_custom_call" | custom-call | flops 268435456 | bytes 1179648 | tf_op jit(solution)/shard_map/mix/pallas_call | solution.py:252
  25.1 1.2 %collective-permute-start.7 = (bf16[512,128]{1,0:T(8,128)(2,1)S(1)}, bf16[512,128]{1,0:T(8,128)(2,1)S(1)}, u32[]{:S(2)}, u32[]{:S(2)}) collective-permute-start(bf16[512,128]{1,0:T(8,128)(2,1)S(1)} %get-tuple-element.19), channel_id=1, source_target_pairs={{0,16},{2,18},{4,20},{6,22},{8,24},{10,26},{12,28},{14,30},{16,0},... | collective-permute-start | bytes 393224 | tf_op jit(solution)/shard_map/ppermute | solution.py:40
  26.3 0.5 %threshold_map.1.refs_6_.refs_4_ = f32[128,512]{1,0:T(8,128)S(1)} custom-call(s32[128,256]{1,0:T(8,128)S(1)} %bitcast.16, f32[8,16]{1,0:T(8,128)S(1)} %copy-done.7), custom_call_target="tpu_custom_call" | custom-call | flops 2097152 | bytes 262144 | tf_op jit(solution)/shard_map/threshold_map/pallas_call | solution.py:221
  26.8 0.7 %collective-permute-done.11.refs_1_ = bf16[512,128]{1,0:T(8,128)(2,1)S(1)} collective-permute-done((bf16[512,128]{1,0:T(8,128)(2,1)S(1)}, bf16[512,128]{1,0:T(8,128)(2,1)S(1)}, u32[]{:S(2)}, u32[]{:S(2)}) %collective-permute-start.11) | collective-permute-done | bytes 131104 | tf_op jit(solution)/shard_map/ppermute | solution.py:40
  27.5 0.1 collective-permute-done.12.refs_2_
  27.6 4.6 %collective-permute-done.13.refs_3_ = bf16[512,128]{1,0:T(8,128)(2,1)S(1)} collective-permute-done((bf16[512,128]{1,0:T(8,128)(2,1)S(1)}, bf16[512,128]{1,0:T(8,128)(2,1)S(1)}, u32[]{:S(2)}, u32[]{:S(2)}) %collective-permute-start.13) | collective-permute-done | bytes 131104 | tf_op jit(solution)/shard_map/ppermute | solution.py:40
  32.3 1.4 %finish.2 = (f32[1024,512]{1,0:T(8,128)}, bf16[1024,512]{1,0:T(8,128)(2,1)}) custom-call(f32[512,128]{1,0:T(8,128)S(1)} %get-tuple-element.22.refs_0_, bf16[512,128]{1,0:T(8,128)(2,1)S(1)} %collective-permute-done.11.refs_1_, bf16[512,128]{1,0:T(8,128)(2,1)S(1)} %collective-permute-done.12.refs_2_, bf16[512,128]{1,0:T(8,128)(2,1)S(1)} %collective-permute-done.13.refs_3_, ...), custom_call_target="tpu_custom_call" | custom-call | flops 134217728 | bytes 2621440 | tf_op jit(solution)/shard_map/finish/pallas_call | solution.py:300
  33.7 0.3 collective-permute-done.7.refs_1_
  34.0 1.4 %finish.3 = (f32[1024,512]{1,0:T(8,128)}, bf16[1024,512]{1,0:T(8,128)(2,1)}) custom-call(f32[512,128]{1,0:T(8,128)S(1)} %get-tuple-element.18.refs_0_, bf16[512,128]{1,0:T(8,128)(2,1)S(1)} %collective-permute-done.7.refs_1_, bf16[1024,512]{1,0:T(8,128)(2,1)S(1)} %bitcast.8, ...), custom_call_target="tpu_custom_call", output_to_operand_aliasing={{0}: (7, {}), {1}: (8, {})} | custom-call | flops 134217728 | bytes 2621440 | tf_op jit(solution)/shard_map/finish/pallas_call | solution.py:300
  (27 shorter events, 0.1 us)
Async XLA Ops:
  0.6 17.8 %copy-start.2 = (bf16[512,64]{0,1:T(8,128)(2,1)S(1)}, bf16[512,64]{0,1:T(8,128)(2,1)}, u32[]{:S(2)}) copy-start(bf16[512,64]{0,1:T(8,128)(2,1)} %param.12) | copy-start | bytes 196612
  0.6 17.8 %copy-start.6 = (bf16[2,2,64,64]{3,2,1,0:T(8,128)(2,1)S(1)}, bf16[2,2,64,64]{3,2,1,0:T(8,128)(2,1)}, u32[]{:S(2)}) copy-start(bf16[2,2,64,64]{3,2,1,0:T(8,128)(2,1)} %ty_ref.1) | copy-start | bytes 98308
  0.7 17.8 %copy-start.3 = (bf16[8,8,64,64]{3,2,1,0:T(8,128)(2,1)S(1)}, bf16[8,8,64,64]{3,2,1,0:T(8,128)(2,1)}, u32[]{:S(2)}) copy-start(bf16[8,8,64,64]{3,2,1,0:T(8,128)(2,1)} %tx_ref.1) | copy-start | bytes 1572868
  2.9 23.3 %copy-start.5 = (s32[8,16,256]{2,1,0:T(8,128)S(1)}, s32[8,16,256]{2,1,0:T(8,128)}, u32[]{:S(2)}) copy-start(s32[8,16,256]{2,1,0:T(8,128)} %param.11) | copy-start | bytes 393220
  2.9 23.3 %copy-start.7 = (f32[8,16]{1,0:T(8,128)S(1)}, f32[8,16]{1,0:T(8,128)}, u32[]{:S(2)}) copy-start(f32[8,16]{1,0:T(8,128)} %threshold_ref.1) | copy-start | bytes 1540
  3.0 10.6 %collective-permute-start.9 = (bf16[512,128]{1,0:T(8,128)(2,1)S(1)}, bf16[512,128]{1,0:T(8,128)(2,1)S(1)}, u32[]{:S(2)}, u32[]{:S(2)}) collective-permute-start(bf16[512,128]{1,0:T(8,128)(2,1)S(1)} %get-tuple-element.20.refs_0_), channel_id=1, source_target_pairs={{0,16},{2,18},{4,20},{6,22},{8,24},{10,26},{12,28},{14,30},{16,0},... | collective-permute-start | bytes 393224 | tf_op jit(solution)/shard_map/ppermute | solution.py:40
  7.1 6.4 %collective-permute-start.8 = (bf16[512,128]{1,0:T(8,128)(2,1)S(1)}, bf16[512,128]{1,0:T(8,128)(2,1)S(1)}, u32[]{:S(2)}, u32[]{:S(2)}) collective-permute-start(bf16[512,128]{1,0:T(8,128)(2,1)S(1)} %get-tuple-element.20.refs_0_), channel_id=1, source_target_pairs={{0,4},{2,6},{4,0},{6,2},{8,12},{10,14},{12,8},{14,10},{16,20},{18,... | collective-permute-start | bytes 393224 | tf_op jit(solution)/shard_map/ppermute | solution.py:40
  7.1 25.2 %copy-start = (bf16[8,8,16,512]{3,2,1,0:T(8,128)(2,1)S(1)}, bf16[8,8,16,512]{3,2,1,0:T(8,128)(2,1)}, u32[]{:S(2)}) copy-start(bf16[8,8,16,512]{3,2,1,0:T(8,128)(2,1)} %param.9) | copy-start | bytes 3145732
  7.1 25.2 %copy-start.1 = (bf16[8,8,16,512]{3,2,1,0:T(8,128)(2,1)S(1)}, bf16[8,8,16,512]{3,2,1,0:T(8,128)(2,1)}, u32[]{:S(2)}) copy-start(bf16[8,8,16,512]{3,2,1,0:T(8,128)(2,1)} %param.8) | copy-start | bytes 3145732
  7.1 25.2 %copy-start.4 = (bf16[64,512]{1,0:T(8,128)(2,1)S(1)}, bf16[64,512]{1,0:T(8,128)(2,1)}, u32[]{:S(2)}) copy-start(bf16[64,512]{1,0:T(8,128)(2,1)} %refs_5_.1) | copy-start | bytes 196612
  7.1 9.0 %collective-permute-start.5 = (bf16[512,128]{1,0:T(8,128)(2,1)S(1)}, bf16[512,128]{1,0:T(8,128)(2,1)S(1)}, u32[]{:S(2)}, u32[]{:S(2)}) collective-permute-start(bf16[512,128]{1,0:T(8,128)(2,1)S(1)} %get-tuple-element.16.refs_0_), channel_id=1, source_target_pairs={{0,10},{2,8},{4,14},{6,12},{8,2},{10,0},{12,6},{14,4},{16,26},{18,... | collective-permute-start | bytes 393224 | tf_op jit(solution)/shard_map/ppermute | solution.py:40
  9.7 7.4 %collective-permute-start.3 = (bf16[512,128]{1,0:T(8,128)(2,1)S(1)}, bf16[512,128]{1,0:T(8,128)(2,1)S(1)}, u32[]{:S(2)}, u32[]{:S(2)}) collective-permute-start(bf16[512,128]{1,0:T(8,128)(2,1)S(1)} %get-tuple-element.16.refs_0_), channel_id=1, source_target_pairs={{0,2},{2,0},{4,6},{6,4},{8,10},{10,8},{12,14},{14,12},{16,18},{18,... | collective-permute-start | bytes 393224 | tf_op jit(solution)/shard_map/ppermute | solution.py:40
  10.2 8.2 %collective-permute-start.1 = (bf16[512,128]{1,0:T(8,128)(2,1)S(1)}, bf16[512,128]{1,0:T(8,128)(2,1)S(1)}, u32[]{:S(2)}, u32[]{:S(2)}) collective-permute-start(bf16[512,128]{1,0:T(8,128)(2,1)S(1)} %get-tuple-element.16.refs_0_), channel_id=1, source_target_pairs={{0,8},{2,10},{4,12},{6,14},{8,0},{10,2},{12,4},{14,6},{16,24},{18,... | collective-permute-start | bytes 393224 | tf_op jit(solution)/shard_map/ppermute | solution.py:40
  13.5 7.1 %collective-permute-start.10 = (bf16[512,128]{1,0:T(8,128)(2,1)S(1)}, bf16[512,128]{1,0:T(8,128)(2,1)S(1)}, u32[]{:S(2)}, u32[]{:S(2)}) collective-permute-start(bf16[512,128]{1,0:T(8,128)(2,1)S(1)} %collective-permute-done.9.refs_2_), channel_id=1, source_target_pairs={{0,4},{2,6},{4,0},{6,2},{8,12},{10,14},{12,8},{14,10},{16,20},{18,... | collective-permute-start | bytes 393224 | tf_op jit(solution)/shard_map/ppermute | solution.py:40
  13.5 8.2 %collective-permute-start = (bf16[512,128]{1,0:T(8,128)(2,1)S(1)}, bf16[512,128]{1,0:T(8,128)(2,1)S(1)}, u32[]{:S(2)}, u32[]{:S(2)}) collective-permute-start(bf16[512,128]{1,0:T(8,128)(2,1)S(1)} %get-tuple-element.16.refs_0_), channel_id=1, source_target_pairs={{0,4},{2,6},{4,0},{6,2},{8,12},{10,14},{12,8},{14,10},{16,20},{18,... | collective-permute-start | bytes 393224 | tf_op jit(solution)/shard_map/ppermute | solution.py:40
  16.1 6.2 %collective-permute-start.6 = (bf16[512,128]{1,0:T(8,128)(2,1)S(1)}, bf16[512,128]{1,0:T(8,128)(2,1)S(1)}, u32[]{:S(2)}, u32[]{:S(2)}) collective-permute-start(bf16[512,128]{1,0:T(8,128)(2,1)S(1)} %collective-permute-done.5.refs_6_), channel_id=1, source_target_pairs={{0,4},{2,6},{4,0},{6,2},{8,12},{10,14},{12,8},{14,10},{16,20},{18,... | collective-permute-start | bytes 393224 | tf_op jit(solution)/shard_map/ppermute | solution.py:40
  17.1 7.6 %collective-permute-start.4 = (bf16[512,128]{1,0:T(8,128)(2,1)S(1)}, bf16[512,128]{1,0:T(8,128)(2,1)S(1)}, u32[]{:S(2)}, u32[]{:S(2)}) collective-permute-start(bf16[512,128]{1,0:T(8,128)(2,1)S(1)} %collective-permute-done.3.refs_4_), channel_id=1, source_target_pairs={{0,4},{2,6},{4,0},{6,2},{8,12},{10,14},{12,8},{14,10},{16,20},{18,... | collective-permute-start | bytes 393224 | tf_op jit(solution)/shard_map/ppermute | solution.py:40
  18.4 6.3 %collective-permute-start.2 = (bf16[512,128]{1,0:T(8,128)(2,1)S(1)}, bf16[512,128]{1,0:T(8,128)(2,1)S(1)}, u32[]{:S(2)}, u32[]{:S(2)}) collective-permute-start(bf16[512,128]{1,0:T(8,128)(2,1)S(1)} %collective-permute-done.1.refs_2_), channel_id=1, source_target_pairs={{0,4},{2,6},{4,0},{6,2},{8,12},{10,14},{12,8},{14,10},{16,20},{18,... | collective-permute-start | bytes 393224 | tf_op jit(solution)/shard_map/ppermute | solution.py:40
  21.1 6.4 %collective-permute-start.11 = (bf16[512,128]{1,0:T(8,128)(2,1)S(1)}, bf16[512,128]{1,0:T(8,128)(2,1)S(1)}, u32[]{:S(2)}, u32[]{:S(2)}) collective-permute-start(bf16[512,128]{1,0:T(8,128)(2,1)S(1)} %get-tuple-element.23), channel_id=1, source_target_pairs={{0,8},{2,10},{4,12},{6,14},{8,0},{10,2},{12,4},{14,6},{16,24},{18,... | collective-permute-start | bytes 393224 | tf_op jit(solution)/shard_map/ppermute | solution.py:40
  21.7 5.9 %collective-permute-start.12 = (bf16[512,128]{1,0:T(8,128)(2,1)S(1)}, bf16[512,128]{1,0:T(8,128)(2,1)S(1)}, u32[]{:S(2)}, u32[]{:S(2)}) collective-permute-start(bf16[512,128]{1,0:T(8,128)(2,1)S(1)} %get-tuple-element.24), channel_id=1, source_target_pairs={{0,2},{2,0},{4,6},{6,4},{8,10},{10,8},{12,14},{14,12},{16,18},{18,... | collective-permute-start | bytes 393224 | tf_op jit(solution)/shard_map/ppermute | solution.py:40
  22.3 10.0 %collective-permute-start.13 = (bf16[512,128]{1,0:T(8,128)(2,1)S(1)}, bf16[512,128]{1,0:T(8,128)(2,1)S(1)}, u32[]{:S(2)}, u32[]{:S(2)}) collective-permute-start(bf16[512,128]{1,0:T(8,128)(2,1)S(1)} %get-tuple-element.25), channel_id=1, source_target_pairs={{0,10},{2,8},{4,14},{6,12},{8,2},{10,0},{12,6},{14,4},{16,26},{18,... | collective-permute-start | bytes 393224 | tf_op jit(solution)/shard_map/ppermute | solution.py:40
  25.1 8.9 %collective-permute-start.7 = (bf16[512,128]{1,0:T(8,128)(2,1)S(1)}, bf16[512,128]{1,0:T(8,128)(2,1)S(1)}, u32[]{:S(2)}, u32[]{:S(2)}) collective-permute-start(bf16[512,128]{1,0:T(8,128)(2,1)S(1)} %get-tuple-element.19), channel_id=1, source_target_pairs={{0,16},{2,18},{4,20},{6,22},{8,24},{10,26},{12,28},{14,30},{16,0},... | collective-permute-start | bytes 393224 | tf_op jit(solution)/shard_map/ppermute | solution.py:40

commit v2 on v1

--- a/solution.py
+++ b/solution.py
@@ -9,6 +9,7 @@
 
 
 SIZES = (1, 1)
+CUTS = (0, 1)
 F32 = jnp.float32
 BF16 = jnp.bfloat16
 
@@ -231,40 +232,63 @@
     )(support, threshold)
 
 
-def mix_kernel(count, *refs):
-    tables_ref, own_ref = refs[count : count + 2]
-    sent = refs[count + 2 :]
+def head_kernel(count, *refs):
+    tables_ref, sum_ref = refs[count:]
     k2 = refs[0].shape[1]
-    rows = refs[0].shape[0]
-    tables = tables_ref[...].reshape(count * k2, tables_ref.shape[2])
-    for i in range(0, rows, 256):
-        here = slice(i, min(i + 256, rows))
-        mixed = mm(jnp.concatenate([ref[here] for ref in refs[:count]], axis=1), tables)
+    tables = tables_ref[:count].reshape(count * k2, tables_ref.shape[2])
+    sum_ref[...] = mm(jnp.concatenate([ref[...] for ref in refs[:count]], axis=1), tables)
+
+
+def tail_kernel(cuts, sum_ref, part_ref, tables_ref, own_ref, *sent):
+    rows, k2 = part_ref.shape
+    size = rows // cuts
+    table = tables_ref[tables_ref.shape[0] - 1]
+    for i in range(0, rows, size):
+        here = slice(i, i + size)
+        mixed = sum_ref[here] + mm(part_ref[here], table)
         own_ref[here] = mixed[:, :k2]
-        for j, out_ref in enumerate(sent):
-            out_ref[here] = mixed[:, (j + 1) * k2 : (j + 2) * k2].astype(BF16)
-
-
-def mix(parts, tables):
+        for j in range(table.shape[1] // k2 - 1):
+            sent[j * cuts + i // size][...] = mixed[:, (j + 1) * k2 : (j + 2) * k2].astype(BF16)
+
+
+def mix_head(parts, tables):
     rows, k2 = parts[0].shape
-    count = len(parts)
+    count, width = len(parts), tables.shape[2]
+    return pl.pallas_call(
+        functools.partial(head_kernel, count),
+        in_specs=[VMEM] * (count + 1),
+        out_specs=VMEM,
+        out_shape=pltpu.VMEM((rows, width), F32),
+        cost_estimate=pl.CostEstimate(
+            flops=2 * rows * count * k2 * width,
+            bytes_accessed=2 * rows * (k2 * count + 2 * width),
+            transcendentals=0,
+        ),
+        compiler_params=PARAMS,
+        name="mix_head",
+    )(*parts, tables)
+
+
+def mix_tail(sums, part, tables, cuts=1):
+    rows, k2 = part.shape
     others = tables.shape[2] // k2 - 1
     return pl.pallas_call(
-        functools.partial(mix_kernel, count),
-        in_specs=[VMEM] * (count + 1),
-        out_specs=[VMEM] * (1 + others),
-        out_shape=[pltpu.VMEM((rows, k2), F32)] + [pltpu.VMEM((rows, k2), BF16)] * others,
-        cost_estimate=pl.CostEstimate(
-            flops=2 * rows * count * k2 * tables.shape[2],
-            bytes_accessed=2 * rows * k2 * (count + others),
+        functools.partial(tail_kernel, cuts),
+        in_specs=[VMEM] * 3,
+        out_specs=[VMEM] * (1 + others * cuts),
+        out_shape=[pltpu.VMEM((rows, k2), F32)]
+        + [pltpu.VMEM((rows // cuts, k2), BF16)] * (others * cuts),
+        cost_estimate=pl.CostEstimate(
+            flops=2 * rows * k2 * tables.shape[2],
+            bytes_accessed=2 * rows * (k2 + 2 * tables.shape[2]),
             transcendentals=0,
         ),
         compiler_params=PARAMS,
-        name="mix",
-    )(*parts, tables)
-
-
-def finish_kernel(first, count, *refs):
+        name="mix_tail",
+    )(sums, part, tables)
+
+
+def finish_kernel(first, skip, count, *refs):
     own_ref, arrived = refs[0], refs[1 : 1 + count]
     model_ref, samples_ref, limit_ref, eval_ref, basis_ref = refs[1 + count : 6 + count]
     next_hbm, residual_hbm, next_ref, residual_ref, sems = refs[-5:]
@@ -275,8 +299,8 @@
     boxes = limit.shape[0]
     copies = []
     for i in range(next_ref.shape[0]):
-        rows, whole = pl.ds(i * boxes, boxes), pl.ds(first + i * boxes, boxes)
-        both = own_ref[rows]
+        rows, whole = pl.ds(i * boxes, boxes), pl.ds(first + skip + i * boxes, boxes)
+        both = own_ref[pl.ds(skip + i * boxes, boxes)]
         for ref in arrived:
             both = both + ref[rows].astype(F32)
         both = both.astype(BF16)
@@ -292,13 +316,13 @@
         copy.wait()
 
 
-def finish(own, arrived, model, samples, limit, evals, basis_t, first, earlier):
+def finish(own, arrived, model, samples, limit, evals, basis_t, first, skip, earlier):
     total, width = model.shape
-    rows, k2 = own.shape
+    rows, k2 = arrived[0].shape
     boxes = limit.shape[0]
     pieces = rows // boxes
     return pl.pallas_call(
-        functools.partial(finish_kernel, first, len(arrived)),
+        functools.partial(finish_kernel, first, skip, len(arrived)),
         in_specs=[VMEM] * (6 + len(arrived)) + [ANY] * len(earlier),
         out_specs=[ANY, ANY],
         out_shape=[
@@ -346,17 +370,23 @@
     for mx, my in around:
         part = exchange(first, mx, my) if mx or my else first
         parts += [part, exchange(part, 1, 0)]
-    own_first, far = mix(parts, gather)
-    far_first = exchange(far, near, 0)
+    cuts = len(CUTS) if counts[0] % (boxes * len(CUTS)) == 0 else 1
+    sums = mix_head(parts[:-1], gather)
+    own_first, *far = mix_tail(sums, parts[-1], gather, cuts)
+    far_first = [exchange(x, near, 0) for x in far]
 
     far = exchange(second, near, 0)
     parts = [second, exchange(second, 1, 0), far, exchange(far, 1, 0)]
-    own_second, *sent = mix(parts, scatter)
+    sums = mix_head(parts[:-1], scatter)
+    own_second, *sent = mix_tail(sums, parts[-1], scatter)
     arrived = [exchange(x, mx, my) for x, (mx, my) in zip(sent, around[1:])]
 
     outs = ()
-    outs = finish(own_second, arrived, model, data, limit, eval_basis, basis_t, firsts[1], outs)
-    outs = finish(own_first, [far_first], model, data, limit, eval_basis, basis_t, firsts[0], outs)
+    outs = finish(own_second, arrived, model, data, limit, eval_basis, basis_t, firsts[1], 0, outs)
+    skip = 0
+    for x in far_first:
+        outs = finish(own_first, [x], model, data, limit, eval_basis, basis_t, firsts[0], skip, outs)
+        skip += x.shape[0]
     model_next, residual = outs
     return model_next.reshape(model_prev.shape), residual.reshape(samples.shape)
 

time: 35.5 us -> 36.9 us (1.039)
  starting transfers between devices: 12.9 us -> 14.8 us
  waiting for transfers between devices: 13 us -> 11.2 us
  Pallas kernels: 8.68 us -> 9.98 us
    ppermute x14 -> x15, starting transfers between devices: 12.9 us -> 14.8 us  [swap(): return lax.ppermute(x, axes, pairs)]
    ppermute x14 -> x15, waiting for transfers between devices: 13 us -> 11.2 us  [swap(): return lax.ppermute(x, axes, pairs)]
    pallas_call x4 -> x7, Pallas kernels: 3.67 us -> 4.96 us  [the longest x3 3.62 us: finish(): pl.pallas_call(functools.partial(finish_kernel, first, skip, len(arrived)...]
  transfers between devices with their start and end apart: 14 -> 15, of which waited for: 8 -> 4; matrix products, arithmetic and copies ran while one was open for 0% -> 0% of each run, Pallas kernels for 14% -> 18%
where the time goes in v2:
time: 36.9 us; the launch traced here: 36.8 us
  starting transfers between devices  14.8 us (40%)
  waiting for transfers between devices  11.2 us (30%)
  Pallas kernels  9.98 us (27%)
  between operations  0.82 us (2%)
    ppermute x15, starting transfers between devices, swap(): return lax.ppermute(x, axes, pairs)  14.8 us
    ppermute x15, waiting for transfers between devices, swap(): return lax.ppermute(x, axes, pairs)  11.2 us
    pallas_call x3, Pallas kernels, finish(): pl.pallas_call(functools.partial(finish_kernel, first, skip, len(arrived)...  3.62 us
    pallas_call x1, Pallas kernels, coefficients(): pl.pallas_call(functools.partial(coeff_kernel, len(counts)), in_specs=[AN...  2.27 us
    pallas_call x1, Pallas kernels, make_tables(): pl.pallas_call(functools.partial(table_kernel, n_gy, near), in_specs=[VME...  2.23 us
    pallas_call x2, Pallas kernels, mix_head(): pl.pallas_call(functools.partial(head_kernel, count), in_specs=[VMEM] * (...  0.86 us
  transfers between devices with their start and end apart: 15, of which 4 were waited for; matrix products, arithmetic and copies ran while one was open for 0% of the time, Pallas kernels for 18%

profile of v2, /device:TPU:0, one launch (start us, length us, event | category | flops | bytes accessed | tf_op | source)
XLA Modules:
  0.0 36.8 jit_solution(6710775409163507106)
XLA Ops:
  0.7 2.3 %coefficients.1 = (bf16[512,128]{1,0:T(8,128)(2,1)S(1)}, bf16[512,128]{1,0:T(8,128)(2,1)S(1)}) custom-call(bf16[1024,512]{1,0:T(8,128)(2,1)} %bitcast.6, bf16[1024,512]{1,0:T(8,128)(2,1)} %bitcast.10, bf16[64,512]{1,0:T(8,128)(2,1)} %refs_5_.3, bf16[64,512]{1,0:T(8,128)(2,1)} %bitcast.14), custom_call_target="tpu_custom_call" | custom-call | flops 268435456 | bytes 2359296 | tf_op jit(solution)/shard_map/coefficients/pallas_call | solution.py:90
  2.9 4.1 %collective-permute-start.10 = (bf16[512,128]{1,0:T(8,128)(2,1)S(1)}, bf16[512,128]{1,0:T(8,128)(2,1)S(1)}, u32[]{:S(2)}, u32[]{:S(2)}) collective-permute-start(bf16[512,128]{1,0:T(8,128)(2,1)S(1)} %get-tuple-element.24.refs_0_), channel_id=1, source_target_pairs={{0,16},{2,18},{4,20},{6,22},{8,24},{10,26},{12,28},{14,30},{16,0},... | collective-permute-start | bytes 393224 | tf_op jit(solution)/shard_map/ppermute | solution.py:41
  7.1 1.5 %collective-permute-start.3 = (bf16[512,128]{1,0:T(8,128)(2,1)S(1)}, bf16[512,128]{1,0:T(8,128)(2,1)S(1)}, u32[]{:S(2)}, u32[]{:S(2)}) collective-permute-start(bf16[512,128]{1,0:T(8,128)(2,1)S(1)} %get-tuple-element.19.refs_0_), channel_id=1, source_target_pairs={{0,2},{2,0},{4,6},{6,4},{8,10},{10,8},{12,14},{14,12},{16,18},{18,... | collective-permute-start | bytes 393224 | tf_op jit(solution)/shard_map/ppermute | solution.py:41
  8.6 1.6 %collective-permute-start.1 = (bf16[512,128]{1,0:T(8,128)(2,1)S(1)}, bf16[512,128]{1,0:T(8,128)(2,1)S(1)}, u32[]{:S(2)}, u32[]{:S(2)}) collective-permute-start(bf16[512,128]{1,0:T(8,128)(2,1)S(1)} %get-tuple-element.19.refs_0_), channel_id=1, source_target_pairs={{0,8},{2,10},{4,12},{6,14},{8,0},{10,2},{12,4},{14,6},{16,24},{18,... | collective-permute-start | bytes 393224 | tf_op jit(solution)/shard_map/ppermute | solution.py:41
  10.1 0.4 %collective-permute-start.5 = (bf16[512,128]{1,0:T(8,128)(2,1)S(1)}, bf16[512,128]{1,0:T(8,128)(2,1)S(1)}, u32[]{:S(2)}, u32[]{:S(2)}) collective-permute-start(bf16[512,128]{1,0:T(8,128)(2,1)S(1)} %get-tuple-element.19.refs_0_), channel_id=1, source_target_pairs={{0,10},{2,8},{4,14},{6,12},{8,2},{10,0},{12,6},{14,4},{16,26},{18,... | collective-permute-start | bytes 393224 | tf_op jit(solution)/shard_map/ppermute | solution.py:41
  10.6 2.9 %collective-permute-done.10.refs_2_ = bf16[512,128]{1,0:T(8,128)(2,1)S(1)} collective-permute-done((bf16[512,128]{1,0:T(8,128)(2,1)S(1)}, bf16[512,128]{1,0:T(8,128)(2,1)S(1)}, u32[]{:S(2)}, u32[]{:S(2)}) %collective-permute-start.10) | collective-permute-done | bytes 131104 | tf_op jit(solution)/shard_map/ppermute | solution.py:41
  13.5 0.5 %collective-permute-start = (bf16[512,128]{1,0:T(8,128)(2,1)S(1)}, bf16[512,128]{1,0:T(8,128)(2,1)S(1)}, u32[]{:S(2)}, u32[]{:S(2)}) collective-permute-start(bf16[512,128]{1,0:T(8,128)(2,1)S(1)} %get-tuple-element.19.refs_0_), channel_id=1, source_target_pairs={{0,4},{2,6},{4,0},{6,2},{8,12},{10,14},{12,8},{14,10},{16,20},{18,... | collective-permute-start | bytes 393224 | tf_op jit(solution)/shard_map/ppermute | solution.py:41
  14.1 2.1 %collective-permute-done.1.refs_2_ = bf16[512,128]{1,0:T(8,128)(2,1)S(1)} collective-permute-done((bf16[512,128]{1,0:T(8,128)(2,1)S(1)}, bf16[512,128]{1,0:T(8,128)(2,1)S(1)}, u32[]{:S(2)}, u32[]{:S(2)}) %collective-permute-start.1) | collective-permute-done | bytes 131104 | tf_op jit(solution)/shard_map/ppermute | solution.py:41
  16.2 2.5 %collective-permute-done.5.refs_6_ = bf16[512,128]{1,0:T(8,128)(2,1)S(1)} collective-permute-done((bf16[512,128]{1,0:T(8,128)(2,1)S(1)}, bf16[512,128]{1,0:T(8,128)(2,1)S(1)}, u32[]{:S(2)}, u32[]{:S(2)}) %collective-permute-start.5) | collective-permute-done | bytes 131104 | tf_op jit(solution)/shard_map/ppermute | solution.py:41
  18.7 2.2 %tables.1 = (bf16[8,128,256]{2,1,0:T(8,128)(2,1)S(1)}, bf16[4,128,512]{2,1,0:T(8,128)(2,1)S(1)}) custom-call(bf16[8,8,64,64]{3,2,1,0:T(8,128)(2,1)S(1)} %copy-done.4, bf16[2,2,64,64]{3,2,1,0:T(8,128)(2,1)S(1)} %copy-done.6, bf16[64,512]{1,0:T(8,128)(2,1)S(1)} %bitcast.15), custom_call_target="tpu_custom_call" | custom-call | flops 200000000 | bytes 2000000 | tf_op jit(solution)/shard_map/tables/pallas_call | solution.py:185
  20.9 0.4 %mix_head.3.sum_ref = f32[512,512]{1,0:T(8,128)S(1)} custom-call(bf16[512,128]{1,0:T(8,128)(2,1)S(1)} %get-tuple-element.24.refs_0_, bf16[512,128]{1,0:T(8,128)(2,1)S(1)} %collective-permute-done.9.refs_1_, bf16[512,128]{1,0:T(8,128)(2,1)S(1)} %collective-permute-done.10.refs_2_, bf16[4,128,512]{2,1,0:T(8,128)(2,1)S(1)} %get-tuple-element.25.refs_3_.tables_ref), custom_call_target="tpu_custom_call" | custom-call | flops 201326592 | bytes 1441792 | tf_op jit(solution)/shard_map/mix_head/pallas_call | solution.py:257
  21.4 0.3 mix_tail.3
  21.7 0.3 collective-permute-start.12
  22.0 1.3 %collective-permute-start.13 = (bf16[512,128]{1,0:T(8,128)(2,1)S(1)}, bf16[512,128]{1,0:T(8,128)(2,1)S(1)}, u32[]{:S(2)}, u32[]{:S(2)}) collective-permute-start(bf16[512,128]{1,0:T(8,128)(2,1)S(1)} %get-tuple-element.28), channel_id=1, source_target_pairs={{0,2},{2,0},{4,6},{6,4},{8,10},{10,8},{12,14},{14,12},{16,18},{18,... | collective-permute-start | bytes 393224 | tf_op jit(solution)/shard_map/ppermute | solution.py:41
  23.3 2.0 %collective-permute-start.14 = (bf16[512,128]{1,0:T(8,128)(2,1)S(1)}, bf16[512,128]{1,0:T(8,128)(2,1)S(1)}, u32[]{:S(2)}, u32[]{:S(2)}) collective-permute-start(bf16[512,128]{1,0:T(8,128)(2,1)S(1)} %get-tuple-element.29), channel_id=1, source_target_pairs={{0,10},{2,8},{4,14},{6,12},{8,2},{10,0},{12,6},{14,4},{16,26},{18,... | collective-permute-start | bytes 393224 | tf_op jit(solution)/shard_map/ppermute | solution.py:41
  25.3 0.4 %mix_head.2.sum_ref = f32[512,256]{1,0:T(8,128)S(1)} custom-call(bf16[512,128]{1,0:T(8,128)(2,1)S(1)} %get-tuple-element.19.refs_0_, bf16[512,128]{1,0:T(8,128)(2,1)S(1)} %collective-permute-done.refs_1_, bf16[512,128]{1,0:T(8,128)(2,1)S(1)} %collective-permute-done.1.refs_2_, bf16[512,128]{1,0:T(8,128)(2,1)S(1)} %collective-permute-done.2.refs_3_, ...), custom_call_target="tpu_custom_call" | custom-call | flops 234881024 | bytes 1441792 | tf_op jit(solution)/shard_map/mix_head/pallas_call | solution.py:257
  25.7 0.2 mix_tail.2
  25.9 1.1 %collective-permute-start.8 = (bf16[256,128]{1,0:T(8,128)(2,1)S(1)}, bf16[256,128]{1,0:T(8,128)(2,1)S(1)}, u32[]{:S(2)}, u32[]{:S(2)}) collective-permute-start(bf16[256,128]{1,0:T(8,128)(2,1)S(1)} %get-tuple-element.23), channel_id=1, source_target_pairs={{0,16},{2,18},{4,20},{6,22},{8,24},{10,26},{12,28},{14,30},{16,0},... | collective-permute-start | bytes 196616 | tf_op jit(solution)/shard_map/ppermute | solution.py:41
  27.1 1.9 %collective-permute-start.7 = (bf16[256,128]{1,0:T(8,128)(2,1)S(1)}, bf16[256,128]{1,0:T(8,128)(2,1)S(1)}, u32[]{:S(2)}, u32[]{:S(2)}) collective-permute-start(bf16[256,128]{1,0:T(8,128)(2,1)S(1)} %get-tuple-element.22), channel_id=1, source_target_pairs={{0,16},{2,18},{4,20},{6,22},{8,24},{10,26},{12,28},{14,30},{16,0},... | collective-permute-start | bytes 196616 | tf_op jit(solution)/shard_map/ppermute | solution.py:41
  28.9 0.5 %threshold_map.1.refs_6_.refs_4_ = f32[128,512]{1,0:T(8,128)S(1)} custom-call(s32[128,256]{1,0:T(8,128)S(1)} %bitcast.19, f32[8,16]{1,0:T(8,128)S(1)} %copy-done.7), custom_call_target="tpu_custom_call" | custom-call | flops 2097152 | bytes 262144 | tf_op jit(solution)/shard_map/threshold_map/pallas_call | solution.py:222
  29.5 3.7 %collective-permute-done.14.refs_3_ = bf16[512,128]{1,0:T(8,128)(2,1)S(1)} collective-permute-done((bf16[512,128]{1,0:T(8,128)(2,1)S(1)}, bf16[512,128]{1,0:T(8,128)(2,1)S(1)}, u32[]{:S(2)}, u32[]{:S(2)}) %collective-permute-start.14) | collective-permute-done | bytes 131104 | tf_op jit(solution)/shard_map/ppermute | solution.py:41
  33.1 1.4 %finish.3 = (f32[1024,512]{1,0:T(8,128)}, bf16[1024,512]{1,0:T(8,128)(2,1)}) custom-call(f32[512,128]{1,0:T(8,128)S(1)} %get-tuple-element.26.refs_0_, bf16[512,128]{1,0:T(8,128)(2,1)S(1)} %collective-permute-done.12.refs_1_, bf16[512,128]{1,0:T(8,128)(2,1)S(1)} %collective-permute-done.13.refs_2_, bf16[512,128]{1,0:T(8,128)(2,1)S(1)} %collective-permute-done.14.refs_3_, ...), custom_call_target="tpu_custom_call" | custom-call | flops 134217728 | bytes 2621440 | tf_op jit(solution)/shard_map/finish/pallas_call | solution.py:324
  34.6 1.1 %finish.4 = (f32[1024,512]{1,0:T(8,128)}, bf16[1024,512]{1,0:T(8,128)(2,1)}) custom-call(f32[512,128]{1,0:T(8,128)S(1)} %get-tuple-element.21.refs_0_, bf16[256,128]{1,0:T(8,128)(2,1)S(1)} %collective-permute-done.8.refs_1_, bf16[1024,512]{1,0:T(8,128)(2,1)S(1)} %bitcast.8, ...), custom_call_target="tpu_custom_call", output_to_operand_aliasing={{0}: (7, {}), {1}: (8, {})} | custom-call | flops 67108864 | bytes 1310720 | tf_op jit(solution)/shard_map/finish/pallas_call | solution.py:324
  35.7 1.1 %finish.5 = (f32[1024,512]{1,0:T(8,128)}, bf16[1024,512]{1,0:T(8,128)(2,1)}) custom-call(f32[512,128]{1,0:T(8,128)S(1)} %get-tuple-element.21.refs_0_, bf16[256,128]{1,0:T(8,128)(2,1)S(1)} %collective-permute-done.7.refs_1_, bf16[1024,512]{1,0:T(8,128)(2,1)S(1)} %bitcast.9, ...), custom_call_target="tpu_custom_call", output_to_operand_aliasing={{0}: (7, {}), {1}: (8, {})} | custom-call | flops 67108864 | bytes 1310720 | tf_op jit(solution)/shard_map/finish/pallas_call | solution.py:324
  (32 shorter events, 0.2 us)
Async XLA Ops:
  0.6 18.0 %copy-start.2 = (bf16[512,64]{0,1:T(8,128)(2,1)S(1)}, bf16[512,64]{0,1:T(8,128)(2,1)}, u32[]{:S(2)}) copy-start(bf16[512,64]{0,1:T(8,128)(2,1)} %param.12) | copy-start | bytes 196612
  0.6 18.0 %copy-start.6 = (bf16[2,2,64,64]{3,2,1,0:T(8,128)(2,1)S(1)}, bf16[2,2,64,64]{3,2,1,0:T(8,128)(2,1)}, u32[]{:S(2)}) copy-start(bf16[2,2,64,64]{3,2,1,0:T(8,128)(2,1)} %ty_ref.1) | copy-start | bytes 98308
  0.7 18.0 %copy-start.4 = (bf16[8,8,64,64]{3,2,1,0:T(8,128)(2,1)S(1)}, bf16[8,8,64,64]{3,2,1,0:T(8,128)(2,1)}, u32[]{:S(2)}) copy-start(bf16[8,8,64,64]{3,2,1,0:T(8,128)(2,1)} %tx_ref.1) | copy-start | bytes 1572868
  2.9 10.6 %collective-permute-start.10 = (bf16[512,128]{1,0:T(8,128)(2,1)S(1)}, bf16[512,128]{1,0:T(8,128)(2,1)S(1)}, u32[]{:S(2)}, u32[]{:S(2)}) collective-permute-start(bf16[512,128]{1,0:T(8,128)(2,1)S(1)} %get-tuple-element.24.refs_0_), channel_id=1, source_target_pairs={{0,16},{2,18},{4,20},{6,22},{8,24},{10,26},{12,28},{14,30},{16,0},... | collective-permute-start | bytes 393224 | tf_op jit(solution)/shard_map/ppermute | solution.py:41
  7.1 6.4 %collective-permute-start.9 = (bf16[512,128]{1,0:T(8,128)(2,1)S(1)}, bf16[512,128]{1,0:T(8,128)(2,1)S(1)}, u32[]{:S(2)}, u32[]{:S(2)}) collective-permute-start(bf16[512,128]{1,0:T(8,128)(2,1)S(1)} %get-tuple-element.24.refs_0_), channel_id=1, source_target_pairs={{0,4},{2,6},{4,0},{6,2},{8,12},{10,14},{12,8},{14,10},{16,20},{18,... | collective-permute-start | bytes 393224 | tf_op jit(solution)/shard_map/ppermute | solution.py:41
  7.1 6.9 %collective-permute-start.3 = (bf16[512,128]{1,0:T(8,128)(2,1)S(1)}, bf16[512,128]{1,0:T(8,128)(2,1)S(1)}, u32[]{:S(2)}, u32[]{:S(2)}) collective-permute-start(bf16[512,128]{1,0:T(8,128)(2,1)S(1)} %get-tuple-element.19.refs_0_), channel_id=1, source_target_pairs={{0,2},{2,0},{4,6},{6,4},{8,10},{10,8},{12,14},{14,12},{16,18},{18,... | collective-permute-start | bytes 393224 | tf_op jit(solution)/shard_map/ppermute | solution.py:41
  8.6 7.6 %collective-permute-start.1 = (bf16[512,128]{1,0:T(8,128)(2,1)S(1)}, bf16[512,128]{1,0:T(8,128)(2,1)S(1)}, u32[]{:S(2)}, u32[]{:S(2)}) collective-permute-start(bf16[512,128]{1,0:T(8,128)(2,1)S(1)} %get-tuple-element.19.refs_0_), channel_id=1, source_target_pairs={{0,8},{2,10},{4,12},{6,14},{8,0},{10,2},{12,4},{14,6},{16,24},{18,... | collective-permute-start | bytes 393224 | tf_op jit(solution)/shard_map/ppermute | solution.py:41
  10.1 8.5 %collective-permute-start.5 = (bf16[512,128]{1,0:T(8,128)(2,1)S(1)}, bf16[512,128]{1,0:T(8,128)(2,1)S(1)}, u32[]{:S(2)}, u32[]{:S(2)}) collective-permute-start(bf16[512,128]{1,0:T(8,128)(2,1)S(1)} %get-tuple-element.19.refs_0_), channel_id=1, source_target_pairs={{0,10},{2,8},{4,14},{6,12},{8,2},{10,0},{12,6},{14,4},{16,26},{18,... | collective-permute-start | bytes 393224 | tf_op jit(solution)/shard_map/ppermute | solution.py:41
  13.5 7.9 %collective-permute-start.11 = (bf16[512,128]{1,0:T(8,128)(2,1)S(1)}, bf16[512,128]{1,0:T(8,128)(2,1)S(1)}, u32[]{:S(2)}, u32[]{:S(2)}) collective-permute-start(bf16[512,128]{1,0:T(8,128)(2,1)S(1)} %collective-permute-done.10.refs_2_), channel_id=1, source_target_pairs={{0,4},{2,6},{4,0},{6,2},{8,12},{10,14},{12,8},{14,10},{16,20},{18,... | collective-permute-start | bytes 393224 | tf_op jit(solution)/shard_map/ppermute | solution.py:41
  13.5 8.5 %collective-permute-start = (bf16[512,128]{1,0:T(8,128)(2,1)S(1)}, bf16[512,128]{1,0:T(8,128)(2,1)S(1)}, u32[]{:S(2)}, u32[]{:S(2)}) collective-permute-start(bf16[512,128]{1,0:T(8,128)(2,1)S(1)} %get-tuple-element.19.refs_0_), channel_id=1, source_target_pairs={{0,4},{2,6},{4,0},{6,2},{8,12},{10,14},{12,8},{14,10},{16,20},{18,... | collective-permute-start | bytes 393224 | tf_op jit(solution)/shard_map/ppermute | solution.py:41
  14.0 9.3 %collective-permute-start.4 = (bf16[512,128]{1,0:T(8,128)(2,1)S(1)}, bf16[512,128]{1,0:T(8,128)(2,1)S(1)}, u32[]{:S(2)}, u32[]{:S(2)}) collective-permute-start(bf16[512,128]{1,0:T(8,128)(2,1)S(1)} %collective-permute-done.3.refs_4_), channel_id=1, source_target_pairs={{0,4},{2,6},{4,0},{6,2},{8,12},{10,14},{12,8},{14,10},{16,20},{18,... | collective-permute-start | bytes 393224 | tf_op jit(solution)/shard_map/ppermute | solution.py:41
  16.2 9.1 %collective-permute-start.2 = (bf16[512,128]{1,0:T(8,128)(2,1)S(1)}, bf16[512,128]{1,0:T(8,128)(2,1)S(1)}, u32[]{:S(2)}, u32[]{:S(2)}) collective-permute-start(bf16[512,128]{1,0:T(8,128)(2,1)S(1)} %collective-permute-done.1.refs_2_), channel_id=1, source_target_pairs={{0,4},{2,6},{4,0},{6,2},{8,12},{10,14},{12,8},{14,10},{16,20},{18,... | collective-permute-start | bytes 393224 | tf_op jit(solution)/shard_map/ppermute | solution.py:41
  18.7 7.1 %collective-permute-start.6 = (bf16[512,128]{1,0:T(8,128)(2,1)S(1)}, bf16[512,128]{1,0:T(8,128)(2,1)S(1)}, u32[]{:S(2)}, u32[]{:S(2)}) collective-permute-start(bf16[512,128]{1,0:T(8,128)(2,1)S(1)} %collective-permute-done.5.refs_6_), channel_id=1, source_target_pairs={{0,4},{2,6},{4,0},{6,2},{8,12},{10,14},{12,8},{14,10},{16,20},{18,... | collective-permute-start | bytes 393224 | tf_op jit(solution)/shard_map/ppermute | solution.py:41
  21.4 7.6 %copy-start.5 = (s32[8,16,256]{2,1,0:T(8,128)S(1)}, s32[8,16,256]{2,1,0:T(8,128)}, u32[]{:S(2)}) copy-start(s32[8,16,256]{2,1,0:T(8,128)} %param.11) | copy-start | bytes 393220
  21.4 7.6 %copy-start.7 = (f32[8,16]{1,0:T(8,128)S(1)}, f32[8,16]{1,0:T(8,128)}, u32[]{:S(2)}) copy-start(f32[8,16]{1,0:T(8,128)} %threshold_ref.1) | copy-start | bytes 1540
  21.7 11.4 %copy-start = (bf16[8,8,16,512]{3,2,1,0:T(8,128)(2,1)S(1)}, bf16[8,8,16,512]{3,2,1,0:T(8,128)(2,1)}, u32[]{:S(2)}) copy-start(bf16[8,8,16,512]{3,2,1,0:T(8,128)(2,1)} %param.9) | copy-start | bytes 3145732
  21.7 11.4 %copy-start.1 = (bf16[8,8,16,512]{3,2,1,0:T(8,128)(2,1)S(1)}, bf16[8,8,16,512]{3,2,1,0:T(8,128)(2,1)}, u32[]{:S(2)}) copy-start(bf16[8,8,16,512]{3,2,1,0:T(8,128)(2,1)} %param.8) | copy-start | bytes 3145732
  21.7 11.4 %copy-start.3 = (bf16[64,512]{1,0:T(8,128)(2,1)S(1)}, bf16[64,512]{1,0:T(8,128)(2,1)}, u32[]{:S(2)}) copy-start(bf16[64,512]{1,0:T(8,128)(2,1)} %refs_5_.3) | copy-start | bytes 196612
  21.7 7.7 %collective-permute-start.12 = (bf16[512,128]{1,0:T(8,128)(2,1)S(1)}, bf16[512,128]{1,0:T(8,128)(2,1)S(1)}, u32[]{:S(2)}, u32[]{:S(2)}) collective-permute-start(bf16[512,128]{1,0:T(8,128)(2,1)S(1)} %get-tuple-element.27), channel_id=1, source_target_pairs={{0,8},{2,10},{4,12},{6,14},{8,0},{10,2},{12,4},{14,6},{16,24},{18,... | collective-permute-start | bytes 393224 | tf_op jit(solution)/shard_map/ppermute | solution.py:41
  22.0 7.5 %collective-permute-start.13 = (bf16[512,128]{1,0:T(8,128)(2,1)S(1)}, bf16[512,128]{1,0:T(8,128)(2,1)S(1)}, u32[]{:S(2)}, u32[]{:S(2)}) collective-permute-start(bf16[512,128]{1,0:T(8,128)(2,1)S(1)} %get-tuple-element.28), channel_id=1, source_target_pairs={{0,2},{2,0},{4,6},{6,4},{8,10},{10,8},{12,14},{14,12},{16,18},{18,... | collective-permute-start | bytes 393224 | tf_op jit(solution)/shard_map/ppermute | solution.py:41
  23.3 9.9 %collective-permute-start.14 = (bf16[512,128]{1,0:T(8,128)(2,1)S(1)}, bf16[512,128]{1,0:T(8,128)(2,1)S(1)}, u32[]{:S(2)}, u32[]{:S(2)}) collective-permute-start(bf16[512,128]{1,0:T(8,128)(2,1)S(1)} %get-tuple-element.29), channel_id=1, source_target_pairs={{0,10},{2,8},{4,14},{6,12},{8,2},{10,0},{12,6},{14,4},{16,26},{18,... | collective-permute-start | bytes 393224 | tf_op jit(solution)/shard_map/ppermute | solution.py:41
  25.9 8.6 %collective-permute-start.8 = (bf16[256,128]{1,0:T(8,128)(2,1)S(1)}, bf16[256,128]{1,0:T(8,128)(2,1)S(1)}, u32[]{:S(2)}, u32[]{:S(2)}) collective-permute-start(bf16[256,128]{1,0:T(8,128)(2,1)S(1)} %get-tuple-element.23), channel_id=1, source_target_pairs={{0,16},{2,18},{4,20},{6,22},{8,24},{10,26},{12,28},{14,30},{16,0},... | collective-permute-start | bytes 196616 | tf_op jit(solution)/shard_map/ppermute | solution.py:41
  27.1 8.6 %collective-permute-start.7 = (bf16[256,128]{1,0:T(8,128)(2,1)S(1)}, bf16[256,128]{1,0:T(8,128)(2,1)S(1)}, u32[]{:S(2)}, u32[]{:S(2)}) collective-permute-start(bf16[256,128]{1,0:T(8,128)(2,1)S(1)} %get-tuple-element.22), channel_id=1, source_target_pairs={{0,16},{2,18},{4,20},{6,22},{8,24},{10,26},{12,28},{14,30},{16,0},... | collective-permute-start | bytes 196616 | tf_op jit(solution)/shard_map/ppermute | solution.py:41
